TPU v7x, 256 devices: a whole 4x4x8 slice. The times are simulated.
256 devices in a mesh: ctx: 8 (over z_hi, core), vocab: 32 (over x, y, z_lo).
Axes of the slice: x: 4, y: 4, z: 8 (z_hi: 4, z_lo: 2; z = z_hi * 2 + z_lo), core: 2. Of those that a mesh axis runs over, the one named last changes fastest.
Arguments:
- hidden: bfloat16 [512, 2, 7168], P('ctx', None, 'vocab'), may hold values from -30 to 30
- head: bfloat16 [7168, 65536], P('ctx', 'vocab'), may hold values from -0.15 to 0.15
- targets: int32 [512, 2], P('ctx'), may hold values from 0 to 65535
- loss_weight: float32 [512, 2], P('ctx'), may hold values from 16 to 256
Outputs:
- token_loss: float32 [512, 2], P('ctx')
- grad_hidden: bfloat16 [512, 2, 7168], P('ctx', None, 'vocab')
All inputs are finite; a program needn't handle non-finite values.
Results may differ from a plain program's by a relative error of at most 0.0046.
Values may be sent and summed in bfloat16 or wider, within the bound.
A program may use at most 64 MiB of HBM per device.

v0:
```python
import jax
import jax.numpy as jnp
from jax import lax
from jax.sharding import PartitionSpec as P


def sent_to_all(x, axis):
    copies = jnp.broadcast_to(x, (lax.axis_size(axis), *x.shape))
    return lax.all_to_all(copies, axis, split_axis=0, concat_axis=0, tiled=True)


def gathered_once(x, axis):
    leaves = jax.tree.leaves(x)
    order = sorted(range(len(leaves)), key=lambda k: -leaves[k].size)
    width = (1, *leaves[order[0]].shape)[-1]
    lines = [
        jnp.pad(leaves[k].reshape(-1), (0, -leaves[k].size % width)).reshape(-1, width)
        for k in order
    ]
    both, at, found = (sent_to_all(jnp.concatenate(lines), axis), 0, {})
    for k, line in zip(order, lines):
        slab = both[:, at : at + len(line)].reshape(len(both), -1)
        found[k] = slab[:, : leaves[k].size].reshape(-1, *leaves[k].shape)
        at += len(line)
    numbers = iter(range(len(leaves)))
    return jax.tree.map(lambda _: found[next(numbers)], x)


def combined_pairwise(pieces, combine):
    while len(jax.tree.leaves(pieces)[0]) > 1:
        pieces = jax.vmap(combine)(
            *(jax.tree.map(lambda part: part[side::2], pieces) for side in (0, 1))
        )
    return jax.tree.map(lambda part: part[0], pieces)


def joined_all(x, axis, combine):
    pieces = gathered_once(x, axis)
    return combined_pairwise(pieces, combine)


def cut_along(x, dim, size):
    lengths = x.shape
    pieces = x.reshape(*lengths[:dim], size, lengths[dim] // size, *lengths[dim + 1 :])
    return jnp.moveaxis(pieces, dim, 0)


def summed_on_arrival(x, axis, dim):
    pieces = cut_along(x, dim, lax.axis_size(axis))
    arrived = lax.all_to_all(pieces, axis, split_axis=0, concat_axis=0, tiled=True)
    return arrived.sum(axis=0)


def combine_stats(first, second):
    first_max, first_sum, first_target = first
    second_max, second_sum, second_target = second
    joined = jnp.maximum(first_max, second_max)
    total = first_sum * jnp.exp(first_max - joined) + second_sum * jnp.exp(second_max - joined)
    return (joined, total, first_target + second_target)


def body(hidden, head, targets, loss_weight):
    group_rows = hidden.shape[0]
    depth_count = hidden.shape[1]
    flat_count = group_rows * depth_count
    ctx_count = lax.axis_size("ctx")
    vocab_count = lax.axis_size("vocab")
    vocab_index = lax.axis_index("vocab")
    vocab_local = head.shape[1]
    flat_hidden = hidden.reshape(flat_count, hidden.shape[2])
    flat_targets = targets.reshape(flat_count)
    flat_weights = loss_weight.reshape(flat_count)
    whole_width = lax.all_gather(flat_hidden, "vocab", axis=1, tiled=True)
    width_slab = lax.all_to_all(whole_width, "ctx", split_axis=1, concat_axis=0, tiled=True)
    logits = lax.psum_scatter(
        jnp.dot(width_slab, head, preferred_element_type=jnp.float32),
        "ctx",
        scatter_dimension=0,
        tiled=True,
    )
    columns = vocab_index * vocab_local + lax.broadcasted_iota(jnp.int32, logits.shape, 1)
    target_hit = columns == flat_targets[:, None]
    local_max = jnp.max(logits, axis=1)
    local_target = jnp.sum(jnp.where(target_hit, logits, 0.0), axis=1)
    local_sum = jnp.sum(jnp.exp(logits - local_max[:, None]), axis=1)
    row_max, sum_exp, target_logit = joined_all(
        (local_max, local_sum, local_target), "vocab", combine_stats
    )
    flat_loss = jnp.log(sum_exp) + row_max - target_logit
    token_loss = flat_loss.reshape(group_rows, depth_count)
    probabilities = jnp.exp(logits - row_max[:, None]) / sum_exp[:, None]
    dlogits = (flat_weights[:, None] * (probabilities - target_hit.astype(jnp.float32))).astype(
        jnp.bfloat16
    )
    grad_slab = lax.dot_general(
        lax.all_gather(dlogits, "ctx", axis=0, tiled=True),
        head,
        (((1,), (1,)), ((), ())),
        preferred_element_type=jnp.float32,
    )
    share_rows = flat_count // vocab_count
    slab_width = grad_slab.shape[1]
    blocks = grad_slab.reshape(ctx_count, vocab_count, share_rows, slab_width)
    reduced = summed_on_arrival(blocks, "vocab", 1).astype(jnp.bfloat16)
    landed = lax.all_to_all(
        lax.all_to_all(reduced, "ctx", split_axis=0, concat_axis=3, tiled=True),
        "vocab",
        split_axis=3,
        concat_axis=1,
        tiled=True,
    )
    grad_out = landed.reshape(group_rows, depth_count, landed.shape[3])
    return (token_loss, grad_out)


def solution(mesh):
    return jax.shard_map(
        body,
        mesh=mesh,
        in_specs=(P("ctx", None, "vocab"), P("ctx", "vocab"), P("ctx", None), P("ctx", None)),
        out_specs=(P("ctx", None), P("ctx", None, "vocab")),
        check_vma=False,
    )
```

profile of v0, /device:TPU:37, one launch (start us, length us, event | category | flops | bytes accessed | tf_op | source)
XLA Modules:
  0.0 561.5 jit_solution(5996300982655620662)
XLA Ops:
  7.2 0.9 reshape.54
  8.1 0.7 copy.29
  8.9 122.1 %all-gather.3.cloned.1.call-done = bf16[128,7168]{0,1:T(8,128)(2,1)} async-done(((bf16[128,224]{0,1:T(8,128)(2,1)}), bf16[128,7168]{0,1:T(8,128)(2,1)}) %all-gather.3.cloned.1.call-update) | async-done | bytes 1835024 | tf_op jit(solution)/shard_map/all_gather | solution.py:73
  131.0 73.4 %all_to_all.62 = bf16[128,8,896]{0,2,1:T(8,128)(2,1)S(1)} all-to-all(bf16[128,8,896]{0,2,1:T(8,128)(2,1)} %bitcast.42), channel_id=1, replica_groups=mesh['ctx'=8,'vocab'=32] {'ctx'}, dimensions={1} | all-to-all | bytes 3670016 | tf_op jit(solution)/shard_map/all_to_all | solution.py:74
  204.4 2.7 copy.30
  207.1 10.3 %fusion.6 = f32[1024,2048]{1,0:T(8,128)} fusion(bf16[1024,896]{1,0:T(8,128)(2,1)} %bitcast.43, bf16[896,2048]{1,0:T(8,128)(2,1)} %param.5), kind=kOutput, calls=%fused_computation.20 | convolution fusion | flops 3758096384 | bytes 13893632 | tf_op jit(solution)/shard_map/dot_general | solution.py:76
  217.5 0.6 copy-done
  218.4 102.2 %reduce-scatter.2.cloned.1.call-done = f32[128,2048]{1,0:T(8,128)} async-done(((f32[1024,2048]{1,0:T(8,128)}), f32[128,2048]{1,0:T(8,128)}) %reduce-scatter.2.cloned.1.call-update) | async-done | bytes 1048592 | tf_op jit(solution)/shard_map/reduce_scatter | solution.py:75
  320.6 1.4 reduce_max.9
  321.9 1.6 exponential_reduce_fusion
  323.6 0.6 broadcast_in_dim.9
  324.2 11.9 %all-to-all-start.1 = ((f32[32,3,128]{2,1,0:T(4,128)}), f32[32,3,128]{2,1,0:T(4,128)S(1)}, u32[]{:S(2)}, u32[]{:S(2)}) async-start(f32[32,3,128]{2,1,0:T(4,128)} %broadcast_in_dim.9), calls=%async_computation.2 | async-start | bytes 131072 | tf_op jit(solution)/shard_map/all_to_all | solution.py:9
  336.3 0.1 mul.54
  336.4 4.4 all-to-all-done.1
  341.5 2.4 fusion.3
  343.9 54.0 %all-gather.5.cloned.1.call-done = bf16[1024,2048]{1,0:T(8,128)(2,1)} async-done(((bf16[128,2048]{1,0:T(8,128)(2,1)}), bf16[1024,2048]{1,0:T(8,128)(2,1)}) %all-gather.5.cloned.1.call-update) | async-done | bytes 4194320 | tf_op jit(solution)/shard_map/all_gather | solution.py:96
  397.9 9.7 %fusion.7 = f32[1024,896]{1,0:T(8,128)} fusion(bf16[1024,2048]{1,0:T(8,128)(2,1)} %all-gather.5.cloned.1.call-done, bf16[896,2048]{1,0:T(8,128)(2,1)} %param.5), kind=kOutput, calls=%fused_computation.21 | convolution fusion | flops 3758096384 | bytes 11534336 | tf_op jit(solution)/shard_map/dot_general | solution.py:95
  407.5 5.0 reshape_reshape.3
  412.6 3.1 copy.46
  415.6 50.4 %all_to_all.63 = f32[32,8,1,4,896]{4,3,1,2,0:T(4,128)} all-to-all(f32[32,8,1,4,896]{4,3,1,2,0:T(4,128)S(1)} %bitcast.38), channel_id=1, replica_groups=mesh['ctx'=8,'vocab'=32] {'vocab'}, dimensions={0} | all-to-all | bytes 7340032 | tf_op jit(solution)/shard_map/all_to_all | solution.py:50
  466.1 2.7 reduce_sum.29
  468.7 12.2 %all_to_all.64 = bf16[8,1,4,896]{3,2,1,0:T(4,128)(2,1)S(1)} all-to-all(bf16[8,1,4,896]{3,2,1,0:T(4,128)(2,1)S(1)} %bitcast.45), channel_id=1, replica_groups=mesh['ctx'=8,'vocab'=32] {'ctx'}, dimensions={0} | all-to-all | bytes 114688 | tf_op jit(solution)/shard_map/all_to_all | solution.py:106
  480.9 6.0 %copy.38 = bf16[1,1,4,7168]{2,1,0,3:T(2,128)(2,1)} copy(bf16[1,1,4,7168]{3,2,1,0:T(4,128)(2,1)S(1)} %bitcast.46) | data formatting | bytes 114688 | tf_op jit(solution)/shard_map/all_to_all | solution.py:106
  486.9 0.5 broadcast.6
  487.4 39.8 %reduce.5 = bf16[7168,4]{1,0:T(8,128)(2,1)S(1)} reduce(bf16[7168,1,1,4]{3,2,1,0:T(2,128)(2,1)} %bitcast.40, bf16[]{:T(256)} %broadcast.6), dimensions={1,2}, to_apply=%bitcast.31.reduce_sub_computation | reduce | bytes 114690
  527.2 2.5 reshape.69
  529.7 6.5 %all-to-all-start.4 = ((bf16[32,2,448]{2,1,0:T(2,128)(2,1)}), bf16[32,2,448]{2,1,0:T(2,128)(2,1)S(1)}, u32[]{:S(2)}, u32[]{:S(2)}) async-start(bf16[32,2,448]{2,1,0:T(2,128)(2,1)} %reshape.69), calls=%async_computation.5 | async-start | bytes 131072 | tf_op jit(solution)/shard_map/all_to_all | solution.py:105
  536.3 0.6 copy.41
  537.0 4.3 all-to-all-done.4
  541.2 5.7 %reshape.70 = bf16[7168,1,1,4]{3,2,1,0:T(2,128)(2,1)} reshape(bf16[32,2,448]{2,1,0:T(2,128)(2,1)S(1)} %all-to-all-done.4) | data formatting | bytes 114688
  546.9 7.1 %copy.39 = bf16[1,1,4,7168]{3,2,1,0:T(4,128)(2,1)S(1)} copy(bf16[1,1,4,7168]{2,1,0,3:T(2,128)(2,1)} %bitcast.39) | data formatting | bytes 114688 | tf_op jit(solution)/shard_map/all_to_all | solution.py:105
  554.3 0.7 reshape.61
  (51 shorter events, 1.3 us)
Async XLA Ops:
  7.2 123.9 %all-gather.3.cloned.1.call-start = ((), (), s32[]{:S(2)}) async-start(), calls=%async_computation.6 | async-start | bytes 1892352 | tf_op jit(solution)/shard_map/all_gather | solution.py:73
  8.9 311.7 %reduce-scatter.2.cloned.1.call-start = ((), (), s32[]{:S(2)}) async-start(), calls=%async_computation.7 | async-start | bytes 9437184 | tf_op jit(solution)/shard_map/reduce_scatter | solution.py:75
  217.4 0.7 copy-start
  217.4 118.8 %copy-start.1 = (f32[64,2]{0,1:T(2,128)S(1)}, f32[64,2]{0,1:T(2,128)}, u32[]{:S(2)}) copy-start(f32[64,2]{0,1:T(2,128)} %param.7) | copy-start | bytes 1540
  324.2 16.7 %all-to-all-start.1 = ((f32[32,3,128]{2,1,0:T(4,128)}), f32[32,3,128]{2,1,0:T(4,128)S(1)}, u32[]{:S(2)}, u32[]{:S(2)}) async-start(f32[32,3,128]{2,1,0:T(4,128)} %broadcast_in_dim.9), calls=%async_computation.2 | async-start | bytes 131072 | tf_op jit(solution)/shard_map/all_to_all | solution.py:9
  336.1 61.7 %all-gather.5.cloned.1.call-start = ((), (), s32[]{:S(2)}) async-start(), calls=%async_computation.8 | async-start | bytes 4718592 | tf_op jit(solution)/shard_map/all_gather | solution.py:96
  529.7 11.6 %all-to-all-start.4 = ((bf16[32,2,448]{2,1,0:T(2,128)(2,1)}), bf16[32,2,448]{2,1,0:T(2,128)(2,1)S(1)}, u32[]{:S(2)}, u32[]{:S(2)}) async-start(bf16[32,2,448]{2,1,0:T(2,128)(2,1)} %reshape.69), calls=%async_computation.5 | async-start | bytes 131072 | tf_op jit(solution)/shard_map/all_to_all | solution.py:105
Sparse Core Ops, SparseCore 0:
  10.3 120.6 all-gather.2
  217.6 102.9 reduce-scatter.1
  344.0 53.7 all-gather.4
where the time goes:
time: 566 us; the launch traced here: 561 us
  waiting for transfers between devices  287 us (51%)
  blocking collectives  136 us (24%)
  other arithmetic  47.9 us (8%)
  local copies, waits for them, and re-layouts  38.1 us (7%)
  matrix products  20 us (4%)
  starting transfers between devices  18.6 us (3%)
  between operations  13.9 us (2%)
    all_gather x1, waiting for transfers between devices, body(): whole_width = lax.all_gather(flat_hidden, 'vocab', axis=1, tiled=True)  122 us
    reduce_scatter x1, waiting for transfers between devices, body(): lax.psum_scatter(jnp.dot(width_slab, head, preferred_element_type=jnp.flo...  102 us
    all_to_all x1, blocking collectives, body(): lax.all_to_all(whole_width, 'ctx', split_axis=1, concat_axis=0, tiled=True)  73.4 us
    all_gather x1, waiting for transfers between devices, body(): lax.all_gather(dlogits, 'ctx', axis=0, tiled=True)  54 us
    all_to_all x1, blocking collectives, summed_on_arrival(): lax.all_to_all(pieces, axis, split_axis=0, concat_axis=0, tiled=True)  50.4 us
    unnamed x1, other arithmetic  39.8 us
    all_to_all x1, blocking collectives, body(): lax.all_to_all(reduced, 'ctx', split_axis=0, concat_axis=3, tiled=True)  12.2 us
    all_to_all x1, starting transfers between devices, sent_to_all(): return lax.all_to_all(copies, axis, split_axis=0, concat_axis=0, tiled=True)  11.9 us
  transfers between devices with their start and end apart: 5, of which 5 were waited for; matrix products, arithmetic and copies ran while one was open for 0% of the time, Pallas kernels for 0%

commit v1 on v0

v1 whole, which is shorter than its diff:
```python
import jax
import jax.numpy as jnp
from jax import lax
from jax.experimental import pallas as pl
from jax.experimental.pallas import tpu as pltpu
from jax.sharding import PartitionSpec as P

F32 = jnp.float32
BF16 = jnp.bfloat16
RING = 4
NV = 32
ROWS = 128
WIDTH = 224
VL = 2048
HV = VL // 2
SLAB = 4 * WIDTH


class Ring4Sum:
    def __init__(self, rdma, base, part, land, plus, minus, add):
        self.rdma, self.base, self.part, self.land = rdma, base, part, land
        self.plus, self.minus, self.add = plus, minus, add

    def copy(self, k):
        d, h, to_plus = ((2, 0, 0), (2, 1, 1), (3, 1, 0), (1, 0, 1), (3, 0, 0), (1, 1, 1))[k]
        dev = self.plus if to_plus else self.minus
        return self.rdma(self.part(d, h), self.land(k), self.base + k, dev)

    def start(self, *which):
        for k in which:
            self.copy(k).start()

    def relay(self):
        self.copy(0).wait_recv()
        self.add(self.part(3, 0), [self.land(0)])
        self.copy(4).start()
        self.copy(1).wait_recv()
        self.add(self.part(1, 1), [self.land(1)])
        self.copy(5).start()

    def arrive(self):
        for k in (2, 3, 4, 5):
            self.copy(k).wait_recv()

    def finish(self):
        self.arrive()
        self.add(self.part(0, 0), [self.land(3), self.land(4)])
        self.add(self.part(0, 1), [self.land(2), self.land(5)])

    def drain(self):
        for k in range(6):
            self.copy(k).wait_send()


def add_into(ref, others):
    total = ref[...]
    for o in others:
        total = total + o[...]
    ref[...] = total


def add_rows(ref, others):
    @pl.loop(0, ref.shape[0] // 16)
    def _(r):
        at = pl.ds(pl.multiple_of(r * 16, 16), 16)
        total = ref[at, :]
        for o in others:
            total = total + o[at, :]
        ref[at, :] = total


def kernel(
    hid,
    head_hbm,
    tgt,
    wgt,
    loss_out,
    grad_out,
    buf,
    head,
    part,
    pair,
    zland,
    logit,
    stat,
    msg,
    peers,
    dl,
    g,
    land1,
    land2,
    zbuf,
    obuf,
    obuf_in,
    ssem,
    rsem,
    st_s,
    st_r,
    lsem,
):
    c = lax.axis_index("ctx")
    v = lax.axis_index("vocab")
    zh, core = c // 2, c % 2
    x, y, zl = v // 8, (v // 2) % 4, v % 2

    def up(i, d):
        return (i + d) % RING

    def dev_zh(d):
        return (up(zh, d) * 2 + core, v)

    def dev_x(d):
        return (c, up(x, d) * 8 + y * 2 + zl)

    def dev_y(d):
        return (c, x * 8 + up(y, d) * 2 + zl)

    partner = (zh * 2 + 1 - core, v)
    dev_zl = (c, x * 8 + y * 2 + 1 - zl)
    swap = (v // 4, 4 * c + v % 4)
    is_self = v // 4 == c
    sv = 4 * c + v % 4

    def rdma(src, dst, i, dev):
        return pltpu.make_async_remote_copy(
            src_ref=src,
            dst_ref=dst,
            send_sem=ssem.at[i],
            recv_sem=rsem.at[i],
            device_id=dev,
            device_id_type=pl.DeviceIdType.MESH,
        )

    head_copy = pltpu.make_async_copy(head_hbm, head, lsem.at[0])
    head_copy.start()

    barrier = pltpu.get_barrier_semaphore()
    for dev in (
        partner,
        dev_zh(1),
        dev_zh(3),
        dev_x(1),
        dev_x(3),
        dev_y(1),
        dev_y(3),
        dev_zl,
    ):
        pl.semaphore_signal(barrier, inc=1, device_id=dev, device_id_type=pl.DeviceIdType.MESH)

    @pl.when(jnp.logical_not(is_self))
    def _():
        pl.semaphore_signal(barrier, inc=1, device_id=swap, device_id_type=pl.DeviceIdType.MESH)
        pl.semaphore_wait(barrier, 9)

    @pl.when(is_self)
    def _():
        pl.semaphore_wait(barrier, 8)

    @pl.when(is_self)
    def _():
        cp = pltpu.make_async_copy(hid, buf.at[x, y, zl], lsem.at[1])
        cp.start()
        cp.wait()

    @pl.when(jnp.logical_not(is_self))
    def _():
        cp = rdma(hid, buf.at[sv // 8, (sv // 2) % 4, sv % 2], 0, swap)
        cp.start()
        cp.wait_send()
        rdma(hid, buf.at[x, y, zl], 0, swap).wait_recv()

    z_out = rdma(buf.at[x, y, zl], buf.at[x, y, zl], 1, dev_zl)
    z_out.start()
    rdma(buf.at[x, y, zl], buf.at[x, y, 1 - zl], 1, dev_zl).wait_recv()

    lines = (
        (lambda a, b: buf.at[a, b, 0], x, y, dev_x, dev_y),
        (lambda a, b: buf.at[b, a, 1], y, x, dev_y, dev_x),
    )
    sends = [z_out]
    for k, (at, a, b, dev_a, dev_b) in enumerate(lines):
        base = 2 + 16 * k
        for d in (1, 3):
            cp = rdma(at(a, b), at(a, b), base + (0 if d == 1 else 1), dev_a(d))
            cp.start()
            sends.append(cp)
    steps = (0, 3, 1, 2)

    def second(k, n):
        at, a, b, dev_a, dev_b = lines[k]
        base = 2 + 16 * k
        for d, o in ((1, 4), (3, 8)):
            tile = at(up(a, steps[n]), b)
            cp = rdma(tile, tile, base + o + n, dev_b(d))
            cp.start()
            sends.append(cp)

    def second_in(k, n, d):
        at, a, b, dev_a, dev_b = lines[k]
        base = 2 + 16 * k
        tile = at(up(a, steps[n]), up(b, -d))
        rdma(tile, tile, base + (4 if d == 1 else 8) + n, dev_b(d)).wait_recv()
        return tile

    for k in (0, 1):
        second(k, 0)
    for k, (at, a, b, dev_a, dev_b) in enumerate(lines):
        base = 2 + 16 * k
        for d, i, rows in ((1, 0, pl.ds(0, 64)), (3, 1, pl.ds(64, 64))):
            tile = at(up(a, -d), b)
            rdma(tile, tile, base + i, dev_a(d)).wait_recv()
            half = tile.at[rows]
            cp = rdma(half, half, base + 2 + i, dev_a(d))
            cp.start()
            sends.append(cp)
            second(k, 1 + i)
    for k, (at, a, b, dev_a, dev_b) in enumerate(lines):
        base = 2 + 16 * k
        for d, i, rows in ((1, 0, pl.ds(0, 64)), (3, 1, pl.ds(64, 64))):
            half = at(up(a, 2), b).at[rows]
            rdma(half, half, base + 2 + i, dev_a(d)).wait_recv()
        second(k, 3)
    for n in (0, 1):
        for k, (at, a, b, dev_a, dev_b) in enumerate(lines):
            tile = second_in(k, n, 1)
            cp = rdma(tile, tile, 2 + 16 * k + 12 + n, dev_b(1))
            cp.start()
            sends.append(cp)
    for n in (2, 3):
        for k, (at, a, b, dev_a, dev_b) in enumerate(lines):
            tile = second_in(k, n, 3)
            cp = rdma(tile, tile, 2 + 16 * k + 12 + n, dev_b(3))
            cp.start()
            sends.append(cp)
    for k, (at, a, b, dev_a, dev_b) in enumerate(lines):
        for n in (2, 3):
            second_in(k, n, 1)
        for n in (0, 1):
            second_in(k, n, 3)
        for n in range(4):
            tile = at(up(a, steps[n]), up(b, 2))
            rdma(tile, tile, 2 + 16 * k + 12 + n, dev_b(1)).wait_recv()
    nsem = 34

    head_copy.wait()

    def forward(d):
        q = up(zh, d)

        @pl.loop(0, VL // 256)
        def _(n):
            cols = pl.ds(pl.multiple_of(n * 256, 256), 256)
            out_cols = pl.ds(pl.multiple_of((n % 4) * 256, 256), 256)
            acc = None
            for j in range(4):
                lhs = jnp.concatenate([buf[q, j // 2, j % 2], buf[q, 2 + j // 2, j % 2]], axis=0)
                term = jnp.dot(
                    lhs, head[j * WIDTH : (j + 1) * WIDTH, cols], preferred_element_type=F32
                )
                acc = term if acc is None else acc + term
            part[q, 0, n // 4, :, out_cols] = acc[:ROWS]
            part[q, 1, n // 4, :, out_cols] = acc[ROWS:]

    def pair_copy(d):
        q = up(zh, d)
        return rdma(part.at[q, 1 - core], pair.at[q], nsem + d, partner)

    def pair_add(d):
        q = up(zh, d)
        pair_copy(d).wait_recv()
        for h in (0, 1):
            add_rows(part.at[q, core, h], [pair.at[q, h]])

    zsum = Ring4Sum(
        rdma,
        nsem + 4,
        lambda d, h: part.at[up(zh, d), core, h],
        lambda k: zland.at[k],
        dev_zh(1),
        dev_zh(3),
        add_rows,
    )
    nsem2 = nsem + 10
    forward(2)
    pair_copy(2).start()
    forward(3)
    pair_copy(3).start()
    pair_add(2)
    zsum.start(0, 1)
    forward(1)
    pair_copy(1).start()
    pair_add(3)
    zsum.start(2)
    pair_add(1)
    zsum.start(3)
    forward(0)
    pair_copy(0).start()
    zsum.relay()
    pair_copy(0).wait_recv()
    zsum.arrive()

    lanes = lax.broadcasted_iota(jnp.int32, (16, 128), 1)
    cols0 = lax.broadcasted_iota(jnp.int32, (16, HV), 1) + v * VL

    @pl.loop(0, ROWS // 16)
    def _(r):
        at = pl.ds(pl.multiple_of(r * 16, 16), 16)
        t = tgt[at, :]
        l0 = part[zh, core, 0, at, :] + pair[zh, 0, at, :] + zland[3, at, :] + zland[4, at, :]
        l1 = part[zh, core, 1, at, :] + pair[zh, 1, at, :] + zland[2, at, :] + zland[5, at, :]
        top = jnp.maximum(jnp.max(l0, axis=1, keepdims=True), jnp.max(l1, axis=1, keepdims=True))
        hit = jnp.sum(jnp.where(cols0 == t, l0, 0.0), axis=1, keepdims=True) + jnp.sum(
            jnp.where(cols0 + HV == t, l1, 0.0), axis=1, keepdims=True
        )
        e0 = jnp.exp(l0 - top)
        e1 = jnp.exp(l1 - top)
        total = jnp.sum(e0, axis=1, keepdims=True) + jnp.sum(e1, axis=1, keepdims=True)
        logit[0, at, :] = e0
        logit[1, at, :] = e1
        stat[at, :] = jnp.where(lanes == 0, top, jnp.where(lanes == 1, total, hit))

    msg[...] = jnp.transpose(stat[...])[:8]

    def peer_copy(r):
        return pltpu.make_async_remote_copy(
            src_ref=msg,
            dst_ref=peers.at[r - 1],
            send_sem=st_s.at[r - 1],
            recv_sem=st_r.at[r - 1],
            device_id=(c, (v + r) % NV),
            device_id_type=pl.DeviceIdType.MESH,
        )

    @pl.loop(1, NV)
    def _(r):
        peer_copy(r).start()

    @pl.loop(1, NV)
    def _(r):
        peer_copy(r).wait_recv()

    top, total, hit = msg[0:1, :], msg[1:2, :], msg[2:3, :]
    best = jnp.maximum(top, jnp.max(peers[:, 0, :], axis=0, keepdims=True))
    everyone = total * jnp.exp(top - best) + jnp.sum(
        peers[:, 1, :] * jnp.exp(peers[:, 0, :] - best), axis=0, keepdims=True
    )
    hits = hit + jnp.sum(peers[:, 2, :], axis=0, keepdims=True)
    loss_out[...] = jnp.broadcast_to(jnp.log(everyone) + best - hits, (8, 128))
    scale = jnp.exp(top - best) / everyone
    stat[...] = jnp.transpose(jnp.broadcast_to(scale, (128, 128)))

    @pl.loop(0, ROWS // 16)
    def _(r):
        at = pl.ds(pl.multiple_of(r * 16, 16), 16)
        t = tgt[at, :]
        w = wgt[at, :]
        s = stat[at, 0:1]
        for h in (0, 1):
            one = (cols0 + h * HV == t).astype(F32)
            dl[zh, core, at, h * HV : (h + 1) * HV] = (w * (logit[h, at, :] * s - one)).astype(BF16)

    def across(slot, i, dev):
        return rdma(slot, slot, i, dev)

    own = dl.at[zh, core]
    top_half, low_half = pl.ds(0, 64), pl.ds(64, 64)
    ag = nsem2
    out = [across(own, ag, dev_zh(1)), across(own, ag + 1, dev_zh(3)), across(own, ag + 2, partner)]
    for cp in out:
        cp.start()

    def backward(d):
        q = up(zh, d)
        lhs = jnp.concatenate([dl[q, 0], dl[q, 1]], axis=0)
        for j in range(4):
            res = lax.dot_general(
                lhs,
                head[j * WIDTH : (j + 1) * WIDTH, :],
                (((1,), (1,)), ((), ())),
                preferred_element_type=F32,
            )
            g[q, j // 2, j % 2] = res[:ROWS]
            g[q, 2 + j // 2, j % 2] = res[ROWS:]

    def landed(d, k, i, rows=None):
        slot = dl.at[up(zh, d), k]
        if rows is not None:
            slot = slot.at[rows]
        across(slot, i, partner).wait_recv()
        return slot

    def onward(slot, i, dev):
        cp = across(slot, i, dev)
        cp.start()
        out.append(cp)

    landed(0, 1 - core, ag + 2)
    backward(0)
    slot = landed(3, core, ag)
    onward(slot.at[top_half], ag + 3, dev_zh(1))
    onward(slot, ag + 4, partner)
    slot = landed(1, core, ag + 1)
    onward(slot.at[low_half], ag + 5, dev_zh(3))
    onward(slot, ag + 6, partner)
    landed(3, 1 - core, ag + 4)
    backward(3)
    landed(1, 1 - core, ag + 6)
    backward(1)
    onward(landed(2, core, ag + 3, top_half), ag + 7, partner)
    onward(landed(2, core, ag + 5, low_half), ag + 8, partner)
    landed(2, 1 - core, ag + 7, top_half)
    landed(2, 1 - core, ag + 8, low_half)
    backward(2)

    rs = ag + 9
    first = [
        Ring4Sum(
            rdma,
            rs,
            lambda d, h: g.at[pl.ds(2 * h, 2), up(y, d), 0],
            lambda k: land1.at[0, k],
            dev_y(1),
            dev_y(3),
            add_into,
        ),
        Ring4Sum(
            rdma,
            rs + 6,
            lambda d, h: g.at[up(x, d), pl.ds(2 * h, 2), 1],
            lambda k: land1.at[1, k],
            dev_x(1),
            dev_x(3),
            add_into,
        ),
    ]
    then = [
        Ring4Sum(
            rdma,
            rs + 12,
            lambda d, h: g.at[up(x, d), y, 0, pl.ds(64 * h, 64)],
            lambda k: land2.at[0, k],
            dev_x(1),
            dev_x(3),
            add_into,
        ),
        Ring4Sum(
            rdma,
            rs + 18,
            lambda d, h: g.at[x, up(y, d), 1, pl.ds(64 * h, 64)],
            lambda k: land2.at[1, k],
            dev_y(1),
            dev_y(3),
            add_into,
        ),
    ]
    for stage in (first, then):
        for s in stage:
            s.start(0, 1, 2, 3)
        for s in stage:
            s.relay()
        for s in stage:
            s.finish()
    zi = rs + 24
    z_last = rdma(g.at[x, y, 1 - zl], zbuf, zi, dev_zl)
    z_last.start()
    z_last.wait_recv()
    obuf[...] = (g[x, y, zl] + zbuf[...]).astype(BF16)

    @pl.when(is_self)
    def _():
        cp = pltpu.make_async_copy(obuf, obuf_in, lsem.at[1])
        cp.start()
        cp.wait()

    @pl.when(jnp.logical_not(is_self))
    def _():
        cp = rdma(obuf, obuf_in, zi + 1, swap)
        cp.start()
        cp.wait()

    grad_out[...] = obuf_in[...]

    for cp in sends:
        cp.wait_send()
    for d in range(4):
        pair_copy(d).wait_send()
    zsum.drain()

    @pl.loop(1, NV)
    def _(r):
        peer_copy(r).wait_send()

    for cp in out:
        cp.wait_send()
    for s in first + then:
        s.drain()
    z_last.wait_send()


NSEM = 34 + 10 + 9 + 24 + 2


def body(hidden, head, targets, loss_weight):
    tile = (ROWS, WIDTH)
    vmem = pl.BlockSpec(memory_space=pltpu.VMEM)
    loss, grad = pl.pallas_call(
        kernel,
        out_shape=(
            jax.ShapeDtypeStruct((8, ROWS), F32),
            jax.ShapeDtypeStruct(tile, BF16),
        ),
        in_specs=[vmem, pl.BlockSpec(memory_space=pl.ANY), vmem, vmem],
        out_specs=(vmem, vmem),
        scratch_shapes=[
            pltpu.VMEM((RING, RING, 2, *tile), BF16),
            pltpu.VMEM((SLAB, VL), BF16),
            pltpu.VMEM((RING, 2, 2, ROWS, HV), F32),
            pltpu.VMEM((RING, 2, ROWS, HV), F32),
            pltpu.VMEM((6, ROWS, HV), F32),
            pltpu.VMEM((2, ROWS, HV), F32),
            pltpu.VMEM((ROWS, 128), F32),
            pltpu.VMEM((8, ROWS), F32),
            pltpu.VMEM((NV - 1, 8, ROWS), F32),
            pltpu.VMEM((RING, 2, ROWS, VL), BF16),
            pltpu.VMEM((RING, RING, 2, *tile), F32),
            pltpu.VMEM((2, 6, 2, *tile), F32),
            pltpu.VMEM((2, 6, ROWS // 2, WIDTH), F32),
            pltpu.VMEM(tile, F32),
            pltpu.VMEM(tile, BF16),
            pltpu.VMEM(tile, BF16),
            pltpu.SemaphoreType.DMA((NSEM,)),
            pltpu.SemaphoreType.DMA((NSEM,)),
            pltpu.SemaphoreType.DMA((NV - 1,)),
            pltpu.SemaphoreType.DMA((NV - 1,)),
            pltpu.SemaphoreType.DMA((2,)),
        ],
        compiler_params=pltpu.CompilerParams(
            collective_id=0, has_side_effects=True, vmem_limit_bytes=60 * 1024 * 1024
        ),
        name="mtp_loss",
    )(
        hidden.reshape(tile),
        head,
        targets.reshape(ROWS, 1),
        loss_weight.reshape(ROWS, 1),
    )
    rows, depths = targets.shape
    return loss[0].reshape(rows, depths), grad.reshape(rows, depths, WIDTH)


def solution(mesh):
    return jax.shard_map(
        body,
        mesh=mesh,
        in_specs=(P("ctx", None, "vocab"), P("ctx", "vocab"), P("ctx", None), P("ctx", None)),
        out_specs=(P("ctx", None), P("ctx", None, "vocab")),
        check_vma=False,
    )
```

time: 566 us -> 212 us (0.37)
  waiting for transfers between devices: 287 us -> 0 us
  Pallas kernels: 0 us -> 202 us
  blocking collectives: 136 us -> 0 us
  other arithmetic: 47.9 us -> 0 us
  local copies, waits for them, and re-layouts: 38.1 us -> 7.43 us
  matrix products: 20 us -> 0 us
  starting transfers between devices: 18.6 us -> 0 us
  between operations: 13.9 us -> 0.65 us
    pallas_call x0 -> x1, Pallas kernels: none -> 202 us  [body(): pl.pallas_call(kernel, out_shape=(jax.ShapeDtypeStruct((8, ROWS), F32), j...]
    all_gather x2 -> x0, waiting for transfers between devices: 176 us -> none  [the longest x1 122 us: body(): whole_width = lax.all_gather(flat_hidden, 'vocab', axis=1, tiled=True)]
    all_to_all x3 -> x0, blocking collectives: 136 us -> none  [the longest x1 73.4 us: body(): lax.all_to_all(whole_width, 'ctx', split_axis=1, concat_axis=0, tiled=True)]
    reduce_scatter x1 -> x0, waiting for transfers between devices: 102 us -> none  [body(): lax.psum_scatter(jnp.dot(width_slab, head, preferred_element_type=jnp.flo...]
    unnamed x1 -> x0, other arithmetic: 39.8 us -> none
    dot_general x2 -> x0, matrix products: 20 us -> none  [the longest x1 10.3 us: body(): jnp.dot(width_slab, head, preferred_element_type=jnp.float32)]
    all_to_all x2 -> x0, starting transfers between devices: 18.4 us -> none  [the longest x1 11.9 us: sent_to_all(): return lax.all_to_all(copies, axis, split_axis=0, concat_axis=0, tiled=True)]
    all_to_all x5 -> x0, local copies, waits for them, and re-layouts: 16 us -> none  [the longest x3 7.3 us: body(): lax.all_to_all(lax.all_to_all(reduced, 'ctx', split_axis=0, concat_axis=3...]
  transfers between devices with their start and end apart: 5 -> 0, of which waited for: 5 -> 0; matrix products, arithmetic and copies ran while one was open for 0% -> 0% of each run, Pallas kernels for 0% -> 0%
where the time goes in v1:
time: 212 us; the launch traced here: 210 us
  Pallas kernels  202 us (95%)
  local copies, waits for them, and re-layouts  7.43 us (4%)
    pallas_call x1, Pallas kernels, body(): pl.pallas_call(kernel, out_shape=(jax.ShapeDtypeStruct((8, ROWS), F32), j...  202 us

profile of v1, /device:TPU:37, one launch (start us, length us, event | category | flops | bytes accessed | tf_op | source)
XLA Modules:
  0.0 210.0 jit_solution(13203135719733398047)
XLA Ops:
  0.6 0.8 copy.11
  1.4 0.7 reshape.20.tgt
  2.1 0.8 copy.12
  2.9 0.7 reshape.21.wgt
  3.6 1.5 reshape.16.hid
  5.1 201.9 %mtp_loss.1 = (f32[8,128]{1,0:T(8,128)}, bf16[128,224]{1,0:T(8,128)(2,1)}) custom-call(bf16[128,224]{1,0:T(8,128)(2,1)} %reshape.16.hid, bf16[896,2048]{1,0:T(8,128)(2,1)} %head_hbm.1, s32[128,1]{1,0:T(8,128)} %reshape.20.tgt, f32[128,1]{1,0:T(8,128)} %reshape.21.wgt), custom_call_target="tpu_custom_call" | custom-call | tf_op jit(solution)/shard_map/mtp_loss/pallas_call | solution.py:506
  207.0 0.7 slice_reduce_fusion
  207.7 0.1 reshape_squeeze.3
  207.9 0.6 copy.15
  208.5 1.5 reshape.19

commit v2 on v0

v2 whole, which is shorter than its diff:
```python
import jax
import jax.numpy as jnp
from jax import lax
from jax.experimental import pallas as pl
from jax.experimental.pallas import tpu as pltpu
from jax.sharding import PartitionSpec as P

F32 = jnp.float32
BF16 = jnp.bfloat16
RING = 4
NV = 32
ROWS = 128
WIDTH = 224
VL = 2048
HV = VL // 2
SLAB = 4 * WIDTH
NP = 2
RP = ROWS // NP
I16 = jnp.int16
LEVELS = 32766.0
HOPS = ((2, 0, 0), (2, 1, 1), (3, 1, 0), (1, 0, 1), (3, 0, 0), (1, 1, 1))


class Ring4Sum:
    def __init__(self, k, base, value, tiles, rows, block, coded, sides, plus, minus):
        self.k, self.base, self.value = k, base, value
        self.tiles, self.rows, self.block = tiles, rows, block
        (self.out, self.land), (self.sout, self.sland, self.cols) = coded, sides
        self.plus, self.minus = plus, minus

    def copies(self, i):
        dev = self.plus if HOPS[i][2] else self.minus
        b = self.base + 2 * i
        return (
            self.k.rdma(self.out.at[i], self.land.at[i], b, dev),
            self.k.rdma(self.sout.at[i], self.sland.at[i], b + 1, dev),
        )

    def send(self, i, landed=()):
        d, h, _ = HOPS[i]
        stat = self.k.stat
        lanes = lax.broadcasted_iota(jnp.int32, (self.block, 128), 1)

        @pl.loop(0, self.rows // self.block)
        def _(r):
            at = pl.ds(pl.multiple_of(r * self.block, self.block), self.block)
            side = jnp.zeros((self.block, 128), F32)
            for t in range(self.tiles):
                val = self.value(d, h, t, at)
                for j in landed:
                    val = val + self.decoded(j, t, at)
                low = jnp.min(val, axis=1, keepdims=True)
                high = jnp.max(val, axis=1, keepdims=True)
                middle = 0.5 * low + 0.5 * high
                span = jnp.maximum(0.5 * high - 0.5 * low, 1e-30)
                steps = jnp.clip(jnp.round((val - middle) * (LEVELS / span)), -LEVELS, LEVELS)
                self.out[i, t, at, :] = steps.astype(jnp.int32).astype(I16)
                side = jnp.where(lanes == 2 * t, middle, side)
                side = jnp.where(lanes == 2 * t + 1, span * (1.0 / LEVELS), side)
            stat[at, :] = side

        self.sout[i] = jnp.transpose(stat[...])[:8]
        for cp in self.copies(i):
            cp.start()
            self.k.pending.append(cp)

    def receive(self, i):
        for cp in self.copies(i):
            cp.wait_recv()
        rows = jnp.concatenate([self.sland[i]] * 16, axis=0)
        self.cols[i] = jnp.transpose(rows)

    def decoded(self, i, t, at):
        steps = self.land[i, t, at, :].astype(jnp.int32).astype(F32)
        return steps * self.cols[i, at, 2 * t + 1 : 2 * t + 2] + self.cols[i, at, 2 * t : 2 * t + 1]

    def relay(self):
        self.receive(0)
        self.send(4, (0,))
        self.receive(1)
        self.send(5, (1,))

    def arrive(self):
        for i in (2, 3, 4, 5):
            self.receive(i)

    def total(self, h, t, at):
        i, j = ((3, 4), (2, 5))[h]
        return self.value(0, h, t, at) + self.decoded(i, t, at) + self.decoded(j, t, at)


class Tools:
    def __init__(self, ssem, rsem, stat):
        self.ssem, self.rsem, self.stat, self.pending = ssem, rsem, stat, []

    def rdma(self, src, dst, i, dev):
        return pltpu.make_async_remote_copy(
            src_ref=src,
            dst_ref=dst,
            send_sem=self.ssem.at[i],
            recv_sem=self.rsem.at[i],
            device_id=dev,
            device_id_type=pl.DeviceIdType.MESH,
        )

    def start(self, src, dst, i, dev):
        cp = self.rdma(src, dst, i, dev)
        cp.start()
        self.pending.append(cp)


def kernel(
    hid,
    head_hbm,
    tgt,
    wgt,
    loss_out,
    grad_out,
    buf,
    head,
    part,
    pair,
    zcode,
    logit,
    stat,
    tcol,
    wcol,
    lcol,
    msg,
    peers,
    dl,
    g,
    code1,
    code2,
    sides,
    cols,
    zbuf,
    obuf,
    obuf_in,
    ssem,
    rsem,
    st_s,
    st_r,
    lsem,
):
    c = lax.axis_index("ctx")
    v = lax.axis_index("vocab")
    zh, core = c // 2, c % 2
    x, y, zl = v // 8, (v // 2) % 4, v % 2
    kit = Tools(ssem, rsem, stat)
    rdma, start = kit.rdma, kit.start

    def up(i, d):
        return (i + d) % RING

    def dev_zh(d):
        return (up(zh, d) * 2 + core, v)

    def dev_x(d):
        return (c, up(x, d) * 8 + y * 2 + zl)

    def dev_y(d):
        return (c, x * 8 + up(y, d) * 2 + zl)

    partner = (zh * 2 + 1 - core, v)
    dev_zl = (c, x * 8 + y * 2 + 1 - zl)
    hx, hy = up(x, zh), core * 2 + y % 2
    holder = (v // 4, hx * 8 + hy * 2 + zl)
    owner = (up(x, 4 - zh) * 2 + y // 2, 4 * c + v % 4)
    is_self = jnp.logical_and(holder[0] == c, holder[1] == v)

    head_copy = pltpu.make_async_copy(head_hbm, head, lsem.at[0])
    head_copy.start()

    barrier = pltpu.get_barrier_semaphore()

    def greet(dev):
        pl.semaphore_signal(barrier, inc=1, device_id=dev, device_id_type=pl.DeviceIdType.MESH)

    for dev in (
        partner,
        dev_zh(1),
        dev_zh(3),
        dev_x(1),
        dev_x(3),
        dev_y(1),
        dev_y(3),
        dev_zl,
    ):
        greet(dev)

    @pl.when(jnp.logical_not(is_self))
    def _():
        greet(holder)
        greet(owner)
        pl.semaphore_wait(barrier, 10)

    @pl.when(is_self)
    def _():
        pl.semaphore_wait(barrier, 8)

    @pl.when(is_self)
    def _():
        cp = pltpu.make_async_copy(hid, buf.at[x, y, zl], lsem.at[1])
        cp.start()
        cp.wait()

    @pl.when(jnp.logical_not(is_self))
    def _():
        cp = rdma(hid, buf.at[hx, hy, zl], 0, holder)
        cp.start()
        cp.wait_send()
        rdma(hid, buf.at[x, y, zl], 0, holder).wait_recv()

    start(buf.at[x, y, zl], buf.at[x, y, zl], 1, dev_zl)

    row = lax.broadcasted_iota(jnp.int32, (ROWS, ROWS // 2), 0)
    tok = lax.broadcasted_iota(jnp.int32, (ROWS, ROWS // 2), 1)

    def as_column(pairs):
        both = jnp.where(row % 2 == 1, pairs[1:2, :], pairs[0:1, :])
        return jnp.sum(jnp.where(row // 2 == tok, both, 0.0), axis=1, keepdims=True)

    tcol[...] = as_column(tgt[...].astype(F32)).astype(jnp.int32)
    wcol[...] = as_column(wgt[...])

    rdma(buf.at[x, y, zl], buf.at[x, y, 1 - zl], 1, dev_zl).wait_recv()

    lines = (
        (lambda a, b: buf.at[a, b, 0], x, y, dev_x, dev_y),
        (lambda a, b: buf.at[b, a, 1], y, x, dev_y, dev_x),
    )
    for k, (at, a, b, dev_a, dev_b) in enumerate(lines):
        base = 2 + 16 * k
        for d in (1, 3):
            start(at(a, b), at(a, b), base + (0 if d == 1 else 1), dev_a(d))
    steps = (0, 3, 1, 2)

    def second(k, n):
        at, a, b, dev_a, dev_b = lines[k]
        base = 2 + 16 * k
        for d, o in ((1, 4), (3, 8)):
            tile = at(up(a, steps[n]), b)
            start(tile, tile, base + o + n, dev_b(d))

    def second_in(k, n, d):
        at, a, b, dev_a, dev_b = lines[k]
        base = 2 + 16 * k
        tile = at(up(a, steps[n]), up(b, 4 - d))
        rdma(tile, tile, base + (4 if d == 1 else 8) + n, dev_b(d)).wait_recv()
        return tile

    for k in (0, 1):
        second(k, 0)
    for k, (at, a, b, dev_a, dev_b) in enumerate(lines):
        base = 2 + 16 * k
        for d, i, rows in ((1, 0, pl.ds(0, 64)), (3, 1, pl.ds(64, 64))):
            tile = at(up(a, 4 - d), b)
            rdma(tile, tile, base + i, dev_a(d)).wait_recv()
            half = tile.at[rows]
            start(half, half, base + 2 + i, dev_a(d))
            second(k, 1 + i)
    for k, (at, a, b, dev_a, dev_b) in enumerate(lines):
        base = 2 + 16 * k
        for d, i, rows in ((1, 0, pl.ds(0, 64)), (3, 1, pl.ds(64, 64))):
            half = at(up(a, 2), b).at[rows]
            rdma(half, half, base + 2 + i, dev_a(d)).wait_recv()
        second(k, 3)
    for n, d in ((0, 1), (1, 1), (2, 3), (3, 3)):
        for k, (at, a, b, dev_a, dev_b) in enumerate(lines):
            tile = second_in(k, n, d)
            start(tile, tile, 2 + 16 * k + 12 + n, dev_b(d))
    for k, (at, a, b, dev_a, dev_b) in enumerate(lines):
        for n, d in ((2, 1), (3, 1), (0, 3), (1, 3)):
            second_in(k, n, d)
        for n in range(4):
            tile = at(up(a, steps[n]), up(b, 2))
            rdma(tile, tile, 2 + 16 * k + 12 + n, dev_b(1)).wait_recv()
    sem = 34

    head_copy.wait()

    def forward(d):
        q = up(zh, d)
        at = up(q, zh)

        @pl.loop(0, VL // 256)
        def _(n):
            cs = pl.ds(pl.multiple_of(n * 256, 256), 256)
            out_cs = pl.ds(pl.multiple_of((n % 4) * 256, 256), 256)
            acc = None
            for j in range(4):
                lhs = jnp.concatenate([buf[at, j // 2, j % 2], buf[at, 2 + j // 2, j % 2]], axis=0)
                term = jnp.dot(
                    lhs, head[j * WIDTH : (j + 1) * WIDTH, cs], preferred_element_type=F32
                )
                acc = term if acc is None else acc + term
            for k in range(2):
                for p in range(NP):
                    lo = k * ROWS + p * RP
                    part[q, k, p, n // 4, :, out_cs] = acc[lo : lo + RP]

        for p in range(NP):
            start(part.at[q, 1 - core, p], pair.at[q, p], sem + d * NP + p, partner)

    def pair_in(d, p):
        q = up(zh, d)
        rdma(part.at[q, 1 - core, p], pair.at[q, p], sem + d * NP + p, partner).wait_recv()

    zr = [
        Ring4Sum(
            kit,
            sem + 4 * NP + 12 * p,
            lambda d, h, t, at, p=p: part[up(zh, d), core, p, h, at, :]
            + pair[up(zh, d), p, h, at, :],
            1,
            RP,
            16,
            (zcode.at[p, 0], zcode.at[p, 1]),
            (sides.at[p, 0, 0], sides.at[p, 0, 1], cols.at[0]),
            dev_zh(1),
            dev_zh(3),
        )
        for p in range(NP)
    ]
    forward(2)
    forward(3)
    pair_in(2, 0)
    zr[0].send(0)
    zr[0].send(1)
    forward(1)
    pair_in(3, 0)
    zr[0].send(2)
    pair_in(1, 0)
    zr[0].send(3)
    pair_in(2, 1)
    zr[1].send(0)
    zr[1].send(1)
    forward(0)
    zr[0].relay()
    pair_in(3, 1)
    zr[1].send(2)
    pair_in(1, 1)
    zr[1].send(3)
    zr[1].relay()
    sem2 = sem + 4 * NP + 12 * NP

    lanes = lax.broadcasted_iota(jnp.int32, (16, 128), 1)
    cols0 = lax.broadcasted_iota(jnp.int32, (16, HV), 1) + v * VL

    def peer_copy(p, r):
        return pltpu.make_async_remote_copy(
            src_ref=msg.at[p],
            dst_ref=peers.at[p, r - 1],
            send_sem=st_s.at[p, r - 1],
            recv_sem=st_r.at[p, r - 1],
            device_id=(c, (v + r) % NV),
            device_id_type=pl.DeviceIdType.MESH,
        )

    def softmax(p):
        pair_in(0, p)
        zr[p].arrive()

        @pl.loop(0, RP // 16)
        def _(r):
            at = pl.ds(pl.multiple_of(r * 16, 16), 16)
            t = tcol[pl.ds(pl.multiple_of(p * RP + r * 16, 16), 16), :]
            l0 = zr[p].total(0, 0, at)
            l1 = zr[p].total(1, 0, at)
            top = jnp.maximum(
                jnp.max(l0, axis=1, keepdims=True), jnp.max(l1, axis=1, keepdims=True)
            )
            hit = jnp.sum(jnp.where(cols0 == t, l0, 0.0), axis=1, keepdims=True) + jnp.sum(
                jnp.where(cols0 + HV == t, l1, 0.0), axis=1, keepdims=True
            )
            e0 = jnp.exp(l0 - top)
            e1 = jnp.exp(l1 - top)
            total = jnp.sum(e0, axis=1, keepdims=True) + jnp.sum(e1, axis=1, keepdims=True)
            logit[p, 0, at, :] = e0
            logit[p, 1, at, :] = e1
            stat[at, :] = jnp.where(lanes == 0, top, jnp.where(lanes == 1, total, hit))

        msg[p] = jnp.transpose(stat[...])[:8]

        @pl.loop(1, NV)
        def _(r):
            peer_copy(p, r).start()

    def gradient(p):
        @pl.loop(1, NV)
        def _(r):
            peer_copy(p, r).wait_recv()

        top, total, hit = msg[p, 0:1, :], msg[p, 1:2, :], msg[p, 2:3, :]
        tops = peers[p, :, 0, :]
        best = jnp.maximum(top, jnp.max(tops, axis=0, keepdims=True))
        everyone = total * jnp.exp(top - best) + jnp.sum(
            peers[p, :, 1, :] * jnp.exp(tops - best), axis=0, keepdims=True
        )
        hits = hit + jnp.sum(peers[p, :, 2, :], axis=0, keepdims=True)
        loss = jnp.log(everyone) + best - hits
        scale = jnp.exp(top - best) / everyone
        odd = lax.broadcasted_iota(jnp.int32, (128, 128), 0) % 2 == 1
        lcol[...] = jnp.transpose(jnp.where(odd, loss, scale))
        spot = lax.broadcasted_iota(jnp.int32, (RP, ROWS // 2), 1) * 2
        line = lax.broadcasted_iota(jnp.int32, (RP, ROWS // 2), 0) + p * RP
        for d in (0, 1):
            found = jnp.sum(
                jnp.where(line == spot + d, lcol[:RP, 1:2], 0.0), axis=0, keepdims=True
            )
            loss_out[d : d + 1, :] = found if p == 0 else loss_out[d : d + 1, :] + found

        @pl.loop(0, RP // 16)
        def _(r):
            at = pl.ds(pl.multiple_of(r * 16, 16), 16)
            here = pl.ds(pl.multiple_of(p * RP + r * 16, 16), 16)
            t = tcol[here, :]
            w = wcol[here, :]
            s = lcol[at, 0:1]
            for h in (0, 1):
                one = (cols0 + h * HV == t).astype(F32)
                dl[zh, core, here, h * HV : (h + 1) * HV] = (
                    w * (logit[p, h, at, :] * s - one)
                ).astype(BF16)

    class Gather:
        def __init__(self, p):
            self.p, self.base = p, sem2 + 9 * p
            self.all = pl.ds(p * RP, RP)
            self.first = pl.ds(p * RP, RP // 2)
            self.last = pl.ds(p * RP + RP // 2, RP // 2)

        def go(self, d, k, rows, i, dev):
            slot = dl.at[up(zh, d), k, rows]
            start(slot, slot, self.base + i, dev)

        def come(self, d, k, rows, i):
            slot = dl.at[up(zh, d), k, rows]
            rdma(slot, slot, self.base + i, partner).wait_recv()

        def begin(self):
            self.go(0, core, self.all, 0, dev_zh(1))
            self.go(0, core, self.all, 1, dev_zh(3))
            self.go(0, core, self.all, 2, partner)

        def near(self):
            self.come(3, core, self.all, 0)
            self.go(3, core, self.first, 3, dev_zh(1))
            self.come(1, core, self.all, 1)
            self.go(1, core, self.last, 5, dev_zh(3))
            self.go(3, core, self.all, 4, partner)
            self.go(1, core, self.all, 6, partner)

        def far(self):
            self.come(2, core, self.first, 3)
            self.go(2, core, self.first, 7, partner)
            self.come(2, core, self.last, 5)
            self.go(2, core, self.last, 8, partner)

        def backward(self, d):
            other = 1 - core
            if d == 2:
                self.come(2, other, self.first, 7)
                self.come(2, other, self.last, 8)
            else:
                self.come(d, other, self.all, {0: 2, 3: 4, 1: 6}[d])
            q = up(zh, d)
            at = up(q, zh)
            lhs = jnp.concatenate([dl[q, 0, self.all], dl[q, 1, self.all]], axis=0)
            for j in range(4):
                res = lax.dot_general(
                    lhs,
                    head[j * WIDTH : (j + 1) * WIDTH, :],
                    (((1,), (1,)), ((), ())),
                    preferred_element_type=F32,
                )
                g[at, j // 2, j % 2, self.all] = res[:RP]
                g[at, 2 + j // 2, j % 2, self.all] = res[RP:]

    class Collect:
        def __init__(self, p):
            self.p = p
            base = sem2 + 9 * NP + (48 + 2) * p
            self.base = base

            def here(at, lo=0):
                return pl.ds(pl.multiple_of(p * RP + lo + at.start, 16), at.size)

            self.here = here

            def ring(i, k, value, tiles, rows, code, dev):
                return Ring4Sum(
                    kit,
                    base + 12 * i,
                    value,
                    tiles,
                    rows,
                    16,
                    (code.at[p, k, 0], code.at[p, k, 1]),
                    (sides.at[p, 1 + i, 0], sides.at[p, 1 + i, 1], cols.at[1 + k]),
                    dev(1),
                    dev(3),
                )

            self.one = (
                ring(0, 0, lambda d, h, t, at: g[2 * h + t, up(y, d), 0, here(at), :], 2, RP, code1, dev_y),
                ring(1, 1, lambda d, h, t, at: g[up(x, d), 2 * h + t, 1, here(at), :], 2, RP, code1, dev_x),
            )
            half = RP // 2
            self.two = (
                ring(2, 0, lambda d, h, t, at: g[up(x, d), y, 0, here(at, half * h), :], 1, half, code2, dev_x),
                ring(3, 1, lambda d, h, t, at: g[x, up(y, d), 1, here(at, half * h), :], 1, half, code2, dev_y),
            )

        def begin(self, stage):
            for i in (0, 1, 2, 3):
                for s in stage:
                    s.send(i)

        def relay(self, stage):
            for s in stage:
                s.relay()

        def end_one(self):
            for k, s in enumerate(self.one):
                s.arrive()

                @pl.loop(0, RP // 16)
                def _(r):
                    at = pl.ds(pl.multiple_of(r * 16, 16), 16)
                    for h in (0, 1):
                        for t in (0, 1):
                            val = s.total(h, t, at)
                            if k == 0:
                                g[2 * h + t, y, 0, self.here(at), :] = val
                            else:
                                g[x, 2 * h + t, 1, self.here(at), :] = val

        def end_two(self):
            for k, s in enumerate(self.two):
                s.arrive()

                @pl.loop(0, RP // 32)
                def _(r):
                    at = pl.ds(pl.multiple_of(r * 16, 16), 16)
                    for h in (0, 1):
                        g[x, y, k, self.here(at, RP // 2 * h), :] = s.total(h, 0, at)

            rows = pl.ds(self.p * RP, RP)
            start(g.at[x, y, 1 - zl, rows], zbuf.at[self.p], self.base + 48, dev_zl)

        def out(self):
            rows = pl.ds(self.p * RP, RP)
            rdma(g.at[x, y, 1 - zl, rows], zbuf.at[self.p], self.base + 48, dev_zl).wait_recv()
            obuf[self.p] = (g[x, y, zl, rows] + zbuf[self.p]).astype(BF16)
            src, dst = obuf.at[self.p], obuf_in.at[self.p]

            @pl.when(is_self)
            def _():
                pltpu.make_async_copy(src, dst, lsem.at[2 + self.p]).start()

            @pl.when(jnp.logical_not(is_self))
            def _():
                rdma(src, dst, self.base + 49, owner).start()

        def done(self):
            src, dst = obuf.at[self.p], obuf_in.at[self.p]

            @pl.when(is_self)
            def _():
                pltpu.make_async_copy(src, dst, lsem.at[2 + self.p]).wait()

            @pl.when(jnp.logical_not(is_self))
            def _():
                rdma(src, dst, self.base + 49, owner).wait()

            grad_out[self.p * RP : (self.p + 1) * RP, :] = obuf_in[self.p]

    ga, gb = Gather(0), Gather(1)
    ea, eb = Collect(0), Collect(1)
    softmax(0)
    gradient(0)
    ga.begin()
    softmax(1)
    ga.backward(0)
    gradient(1)
    ga.near()
    gb.begin()
    ga.backward(3)
    ga.backward(1)
    ga.far()
    ga.backward(2)
    ea.begin(ea.one)
    gb.backward(0)
    ea.relay(ea.one)
    gb.near()
    ea.end_one()
    ea.begin(ea.two)
    gb.backward(3)
    ea.relay(ea.two)
    gb.backward(1)
    gb.far()
    ea.end_two()
    gb.backward(2)
    eb.begin(eb.one)
    ea.out()
    eb.relay(eb.one)
    eb.end_one()
    eb.begin(eb.two)
    eb.relay(eb.two)
    eb.end_two()
    eb.out()
    ea.done()
    eb.done()

    for cp in kit.pending:
        cp.wait_send()

    for p in range(NP):

        @pl.loop(1, NV)
        def _(r):
            peer_copy(p, r).wait_send()


NSEM = 34 + 4 * NP + 12 * NP + 9 * NP + 50 * NP


def body(hidden, head, targets, loss_weight):
    tile = (ROWS, WIDTH)
    vmem = pl.BlockSpec(memory_space=pltpu.VMEM)
    loss, grad = pl.pallas_call(
        kernel,
        out_shape=(
            jax.ShapeDtypeStruct((2, ROWS // 2), F32),
            jax.ShapeDtypeStruct(tile, BF16),
        ),
        in_specs=[vmem, pl.BlockSpec(memory_space=pl.ANY), vmem, vmem],
        out_specs=(vmem, vmem),
        scratch_shapes=[
            pltpu.VMEM((RING, RING, 2, *tile), BF16),
            pltpu.VMEM((SLAB, VL), BF16),
            pltpu.VMEM((RING, 2, NP, 2, RP, HV), F32),
            pltpu.VMEM((RING, NP, 2, RP, HV), F32),
            pltpu.VMEM((NP, 2, 6, 1, RP, HV), I16),
            pltpu.VMEM((NP, 2, RP, HV), F32),
            pltpu.VMEM((ROWS, 128), F32),
            pltpu.VMEM((ROWS, 1), jnp.int32),
            pltpu.VMEM((ROWS, 1), F32),
            pltpu.VMEM((ROWS, 128), F32),
            pltpu.VMEM((NP, 8, ROWS), F32),
            pltpu.VMEM((NP, NV - 1, 8, ROWS), F32),
            pltpu.VMEM((RING, 2, ROWS, VL), BF16),
            pltpu.VMEM((RING, RING, 2, *tile), F32),
            pltpu.VMEM((NP, 2, 2, 6, 2, RP, WIDTH), I16),
            pltpu.VMEM((NP, 2, 2, 6, 1, RP // 2, WIDTH), I16),
            pltpu.VMEM((NP, 5, 2, 6, 8, 128), F32),
            pltpu.VMEM((3, 6, 128, 128), F32),
            pltpu.VMEM((NP, RP, WIDTH), F32),
            pltpu.VMEM((NP, RP, WIDTH), BF16),
            pltpu.VMEM((NP, RP, WIDTH), BF16),
            pltpu.SemaphoreType.DMA((NSEM,)),
            pltpu.SemaphoreType.DMA((NSEM,)),
            pltpu.SemaphoreType.DMA((NP, NV - 1)),
            pltpu.SemaphoreType.DMA((NP, NV - 1)),
            pltpu.SemaphoreType.DMA((2 + NP,)),
        ],
        compiler_params=pltpu.CompilerParams(
            collective_id=0, has_side_effects=True, vmem_limit_bytes=60 * 1024 * 1024
        ),
        name="mtp_loss",
    )(hidden.reshape(tile), head, targets.T, loss_weight.T)
    rows, depths = targets.shape
    return loss.T, grad.reshape(rows, depths, WIDTH)


def solution(mesh):
    return jax.shard_map(
        body,
        mesh=mesh,
        in_specs=(P("ctx", None, "vocab"), P("ctx", "vocab"), P("ctx", None), P("ctx", None)),
        out_specs=(P("ctx", None), P("ctx", None, "vocab")),
        check_vma=False,
    )
```

time: 566 us -> 178 us (0.31)
  waiting for transfers between devices: 287 us -> 0 us
  Pallas kernels: 0 us -> 172 us
  blocking collectives: 136 us -> 0 us
  other arithmetic: 47.9 us -> 0 us
  local copies, waits for them, and re-layouts: 38.1 us -> 4.24 us
  matrix products: 20 us -> 0 us
  starting transfers between devices: 18.6 us -> 0 us
  between operations: 13.9 us -> 0.64 us
    all_gather x2 -> x0, waiting for transfers between devices: 176 us -> none  [the longest x1 122 us: body(): whole_width = lax.all_gather(flat_hidden, 'vocab', axis=1, tiled=True)]
    pallas_call x0 -> x1, Pallas kernels: none -> 172 us  [body(): pl.pallas_call(kernel, out_shape=(jax.ShapeDtypeStruct((2, ROWS // 2), F3...]
    all_to_all x3 -> x0, blocking collectives: 136 us -> none  [the longest x1 73.4 us: body(): lax.all_to_all(whole_width, 'ctx', split_axis=1, concat_axis=0, tiled=True)]
    reduce_scatter x1 -> x0, waiting for transfers between devices: 102 us -> none  [body(): lax.psum_scatter(jnp.dot(width_slab, head, preferred_element_type=jnp.flo...]
    unnamed x1 -> x0, other arithmetic: 39.8 us -> none
    dot_general x2 -> x0, matrix products: 20 us -> none  [the longest x1 10.3 us: body(): jnp.dot(width_slab, head, preferred_element_type=jnp.float32)]
    all_to_all x2 -> x0, starting transfers between devices: 18.4 us -> none  [the longest x1 11.9 us: sent_to_all(): return lax.all_to_all(copies, axis, split_axis=0, concat_axis=0, tiled=True)]
    all_to_all x5 -> x0, local copies, waits for them, and re-layouts: 16 us -> none  [the longest x3 7.3 us: body(): lax.all_to_all(lax.all_to_all(reduced, 'ctx', split_axis=0, concat_axis=3...]
  transfers between devices with their start and end apart: 5 -> 0, of which waited for: 5 -> 0; matrix products, arithmetic and copies ran while one was open for 0% -> 0% of each run, Pallas kernels for 0% -> 0%
where the time goes in v2:
time: 178 us; the launch traced here: 177 us
  Pallas kernels  172 us (97%)
  local copies, waits for them, and re-layouts  4.24 us (2%)
    pallas_call x1, Pallas kernels, body(): pl.pallas_call(kernel, out_shape=(jax.ShapeDtypeStruct((2, ROWS // 2), F3...  172 us

profile of v2, /device:TPU:37, one launch (start us, length us, event | category | flops | bytes accessed | tf_op | source)
XLA Modules:
  0.0 177.0 jit_solution(4081172408314997075)
XLA Ops:
  0.6 1.5 reshape.10.hid
  2.2 172.1 %mtp_loss.1 = (f32[2,64]{1,0:T(2,128)}, bf16[128,224]{1,0:T(8,128)(2,1)}) custom-call(bf16[128,224]{1,0:T(8,128)(2,1)} %reshape.10.hid, bf16[896,2048]{1,0:T(8,128)(2,1)} %head_hbm.1, s32[2,64]{1,0:T(2,128)} %bitcast.3, f32[2,64]{1,0:T(2,128)} %bitcast.4), custom_call_target="tpu_custom_call" | custom-call | tf_op jit(solution)/shard_map/mtp_loss/pallas_call | solution.py:633
  174.2 1.5 reshape.11
  175.8 1.2 copy.7

commit v3 on v2

--- a/solution.py
+++ b/solution.py
@@ -41,9 +41,8 @@
         stat = self.k.stat
         lanes = lax.broadcasted_iota(jnp.int32, (self.block, 128), 1)
 
-        @pl.loop(0, self.rows // self.block)
-        def _(r):
-            at = pl.ds(pl.multiple_of(r * self.block, self.block), self.block)
+        for r in range(self.rows // self.block):
+            at = pl.ds(r * self.block, self.block)
             side = jnp.zeros((self.block, 128), F32)
             for t in range(self.tiles):
                 val = self.value(d, h, t, at)
@@ -280,14 +279,14 @@
 
     head_copy.wait()
 
-    def forward(d):
+    def forward(d, h):
         q = up(zh, d)
         at = up(q, zh)
 
-        @pl.loop(0, VL // 256)
+        @pl.loop(0, HV // 256)
         def _(n):
-            cs = pl.ds(pl.multiple_of(n * 256, 256), 256)
-            out_cs = pl.ds(pl.multiple_of((n % 4) * 256, 256), 256)
+            cs = pl.ds(pl.multiple_of(h * HV + n * 256, 256), 256)
+            out_cs = pl.ds(pl.multiple_of(n * 256, 256), 256)
             acc = None
             for j in range(4):
                 lhs = jnp.concatenate([buf[at, j // 2, j % 2], buf[at, 2 + j // 2, j % 2]], axis=0)
@@ -298,19 +297,22 @@
             for k in range(2):
                 for p in range(NP):
                     lo = k * ROWS + p * RP
-                    part[q, k, p, n // 4, :, out_cs] = acc[lo : lo + RP]
+                    part[q, k, p, h, :, out_cs] = acc[lo : lo + RP]
 
         for p in range(NP):
-            start(part.at[q, 1 - core, p], pair.at[q, p], sem + d * NP + p, partner)
-
-    def pair_in(d, p):
+            start(part.at[q, 1 - core, p, h], pair.at[q, p, h], pair_sem(d, p, h), partner)
+
+    def pair_sem(d, p, h):
+        return sem + (d * NP + p) * 2 + h
+
+    def pair_in(d, p, h):
         q = up(zh, d)
-        rdma(part.at[q, 1 - core, p], pair.at[q, p], sem + d * NP + p, partner).wait_recv()
+        rdma(part.at[q, 1 - core, p, h], pair.at[q, p, h], pair_sem(d, p, h), partner).wait_recv()
 
     zr = [
         Ring4Sum(
             kit,
-            sem + 4 * NP + 12 * p,
+            sem + 8 * NP + 12 * p,
             lambda d, h, t, at, p=p: part[up(zh, d), core, p, h, at, :]
             + pair[up(zh, d), p, h, at, :],
             1,
@@ -323,27 +325,35 @@
         )
         for p in range(NP)
     ]
-    forward(2)
-    forward(3)
-    pair_in(2, 0)
-    zr[0].send(0)
-    zr[0].send(1)
-    forward(1)
-    pair_in(3, 0)
+    def logits_begin(p):
+        for h in (0, 1):
+            pair_in(2, p, h)
+            zr[p].send(h)
+
+    forward(2, 0)
+    forward(2, 1)
+    logits_begin(0)
+    forward(3, 1)
+    pair_in(3, 0, 1)
     zr[0].send(2)
-    pair_in(1, 0)
+    forward(1, 0)
+    pair_in(1, 0, 0)
     zr[0].send(3)
-    pair_in(2, 1)
-    zr[1].send(0)
-    zr[1].send(1)
-    forward(0)
+    forward(3, 0)
+    forward(1, 1)
+    pair_in(3, 0, 0)
+    pair_in(1, 0, 1)
     zr[0].relay()
-    pair_in(3, 1)
+    logits_begin(1)
+    pair_in(3, 1, 1)
     zr[1].send(2)
-    pair_in(1, 1)
+    pair_in(1, 1, 0)
     zr[1].send(3)
-    zr[1].relay()
-    sem2 = sem + 4 * NP + 12 * NP
+    forward(0, 0)
+    forward(0, 1)
+    pair_in(3, 1, 0)
+    pair_in(1, 1, 1)
+    sem2 = sem + 8 * NP + 12 * NP
 
     lanes = lax.broadcasted_iota(jnp.int32, (16, 128), 1)
     cols0 = lax.broadcasted_iota(jnp.int32, (16, HV), 1) + v * VL
@@ -359,7 +369,8 @@
         )
 
     def softmax(p):
-        pair_in(0, p)
+        for h in (0, 1):
+            pair_in(0, p, h)
         zr[p].arrive()
 
         @pl.loop(0, RP // 16)
@@ -458,16 +469,16 @@
             self.come(2, core, self.last, 5)
             self.go(2, core, self.last, 8, partner)
 
-        def backward(self, d):
+        def backward(self, *ds):
             other = 1 - core
-            if d == 2:
-                self.come(2, other, self.first, 7)
-                self.come(2, other, self.last, 8)
-            else:
-                self.come(d, other, self.all, {0: 2, 3: 4, 1: 6}[d])
-            q = up(zh, d)
-            at = up(q, zh)
-            lhs = jnp.concatenate([dl[q, 0, self.all], dl[q, 1, self.all]], axis=0)
+            for d in ds:
+                if d == 2:
+                    self.come(2, other, self.first, 7)
+                    self.come(2, other, self.last, 8)
+                else:
+                    self.come(d, other, self.all, {0: 2, 3: 4, 1: 6}[d])
+            lhs = [dl[up(zh, d), k, self.all] for d in ds for k in (0, 1)]
+            lhs = jnp.concatenate(lhs, axis=0)
             for j in range(4):
                 res = lax.dot_general(
                     lhs,
@@ -475,8 +486,11 @@
                     (((1,), (1,)), ((), ())),
                     preferred_element_type=F32,
                 )
-                g[at, j // 2, j % 2, self.all] = res[:RP]
-                g[at, 2 + j // 2, j % 2, self.all] = res[RP:]
+                for i, d in enumerate(ds):
+                    at = up(up(zh, d), zh)
+                    for k in (0, 1):
+                        lo = (2 * i + k) * RP
+                        g[at, 2 * k + j // 2, j % 2, self.all] = res[lo : lo + RP]
 
     class Collect:
         def __init__(self, p):
@@ -485,7 +499,7 @@
             self.base = base
 
             def here(at, lo=0):
-                return pl.ds(pl.multiple_of(p * RP + lo + at.start, 16), at.size)
+                return pl.ds(p * RP + lo + at.start, at.size)
 
             self.here = here
 
@@ -496,7 +510,7 @@
                     value,
                     tiles,
                     rows,
-                    16,
+                    rows,
                     (code.at[p, k, 0], code.at[p, k, 1]),
                     (sides.at[p, 1 + i, 0], sides.at[p, 1 + i, 1], cols.at[1 + k]),
                     dev(1),
@@ -526,26 +540,22 @@
             for k, s in enumerate(self.one):
                 s.arrive()
 
-                @pl.loop(0, RP // 16)
-                def _(r):
-                    at = pl.ds(pl.multiple_of(r * 16, 16), 16)
-                    for h in (0, 1):
-                        for t in (0, 1):
-                            val = s.total(h, t, at)
-                            if k == 0:
-                                g[2 * h + t, y, 0, self.here(at), :] = val
-                            else:
-                                g[x, 2 * h + t, 1, self.here(at), :] = val
+                at = pl.ds(0, RP)
+                for h in (0, 1):
+                    for t in (0, 1):
+                        val = s.total(h, t, at)
+                        if k == 0:
+                            g[2 * h + t, y, 0, self.here(at), :] = val
+                        else:
+                            g[x, 2 * h + t, 1, self.here(at), :] = val
 
         def end_two(self):
             for k, s in enumerate(self.two):
                 s.arrive()
 
-                @pl.loop(0, RP // 32)
-                def _(r):
-                    at = pl.ds(pl.multiple_of(r * 16, 16), 16)
-                    for h in (0, 1):
-                        g[x, y, k, self.here(at, RP // 2 * h), :] = s.total(h, 0, at)
+                at = pl.ds(0, RP // 2)
+                for h in (0, 1):
+                    g[x, y, k, self.here(at, RP // 2 * h), :] = s.total(h, 0, at)
 
             rows = pl.ds(self.p * RP, RP)
             start(g.at[x, y, 1 - zl, rows], zbuf.at[self.p], self.base + 48, dev_zl)
@@ -580,6 +590,7 @@
     ga, gb = Gather(0), Gather(1)
     ea, eb = Collect(0), Collect(1)
     softmax(0)
+    zr[1].relay()
     gradient(0)
     ga.begin()
     softmax(1)
@@ -587,8 +598,7 @@
     gradient(1)
     ga.near()
     gb.begin()
-    ga.backward(3)
-    ga.backward(1)
+    ga.backward(3, 1)
     ga.far()
     ga.backward(2)
     ea.begin(ea.one)
@@ -597,15 +607,14 @@
     gb.near()
     ea.end_one()
     ea.begin(ea.two)
-    gb.backward(3)
+    gb.backward(3, 1)
+    gb.far()
     ea.relay(ea.two)
-    gb.backward(1)
-    gb.far()
-    ea.end_two()
     gb.backward(2)
     eb.begin(eb.one)
+    ea.end_two()
+    eb.relay(eb.one)
     ea.out()
-    eb.relay(eb.one)
     eb.end_one()
     eb.begin(eb.two)
     eb.relay(eb.two)
@@ -624,7 +633,7 @@
             peer_copy(p, r).wait_send()
 
 
-NSEM = 34 + 4 * NP + 12 * NP + 9 * NP + 50 * NP
+NSEM = 34 + 8 * NP + 12 * NP + 9 * NP + 50 * NP
 
 
 def body(hidden, head, targets, loss_weight):

time: 178 us -> 163 us (0.916)
  Pallas kernels: 172 us -> 158 us
    pallas_call x1, Pallas kernels: 172 us -> 158 us  [body(): pl.pallas_call(kernel, out_shape=(jax.ShapeDtypeStruct((2, ROWS // 2), F3...]
where the time goes in v3:
time: 163 us; the launch traced here: 162 us
  Pallas kernels  158 us (97%)
  local copies, waits for them, and re-layouts  4.24 us (3%)
    pallas_call x1, Pallas kernels, body(): pl.pallas_call(kernel, out_shape=(jax.ShapeDtypeStruct((2, ROWS // 2), F3...  158 us

profile of v3, /device:TPU:37, one launch (start us, length us, event | category | flops | bytes accessed | tf_op | source)
XLA Modules:
  0.0 162.5 jit_solution(17658535992688016583)
XLA Ops:
  0.6 1.5 reshape.10.hid
  2.2 157.6 %mtp_loss.1 = (f32[2,64]{1,0:T(2,128)}, bf16[128,224]{1,0:T(8,128)(2,1)}) custom-call(bf16[128,224]{1,0:T(8,128)(2,1)} %reshape.10.hid, bf16[896,2048]{1,0:T(8,128)(2,1)} %head_hbm.1, s32[2,64]{1,0:T(2,128)} %bitcast.3, f32[2,64]{1,0:T(2,128)} %bitcast.4), custom_call_target="tpu_custom_call" | custom-call | tf_op jit(solution)/shard_map/mtp_loss/pallas_call | solution.py:642
  159.8 1.5 reshape.11
  161.3 1.2 copy.7

commit v4 on v3

--- a/solution.py
+++ b/solution.py
@@ -130,7 +130,7 @@
     dl,
     g,
     code1,
-    code2,
+    land2,
     sides,
     cols,
     zbuf,
@@ -495,7 +495,7 @@
     class Collect:
         def __init__(self, p):
             self.p = p
-            base = sem2 + 9 * NP + (48 + 2) * p
+            base = sem2 + 9 * NP + 32 * p
             self.base = base
 
             def here(at, lo=0):
@@ -521,11 +521,19 @@
                 ring(0, 0, lambda d, h, t, at: g[2 * h + t, up(y, d), 0, here(at), :], 2, RP, code1, dev_y),
                 ring(1, 1, lambda d, h, t, at: g[up(x, d), 2 * h + t, 1, here(at), :], 2, RP, code1, dev_x),
             )
-            half = RP // 2
-            self.two = (
-                ring(2, 0, lambda d, h, t, at: g[up(x, d), y, 0, here(at, half * h), :], 1, half, code2, dev_x),
-                ring(3, 1, lambda d, h, t, at: g[x, up(y, d), 1, here(at, half * h), :], 1, half, code2, dev_y),
-            )
+
+        def straight(self, k, d):
+            rows = pl.ds(self.p * RP, RP)
+            if k == 0:
+                src, dev = g.at[up(x, d), y, 0, rows], dev_x(d)
+            else:
+                src, dev = g.at[x, up(y, d), 1, rows], dev_y(d)
+            return src, land2.at[self.p, k, d - 1], self.base + 24 + 3 * k + d - 1, dev
+
+        def begin_two(self):
+            for d in (2, 1, 3):
+                for k in (0, 1):
+                    start(*self.straight(k, d))
 
         def begin(self, stage):
             for i in (0, 1, 2, 3):
@@ -550,19 +558,22 @@
                             g[x, 2 * h + t, 1, self.here(at), :] = val
 
         def end_two(self):
-            for k, s in enumerate(self.two):
-                s.arrive()
-
-                at = pl.ds(0, RP // 2)
-                for h in (0, 1):
-                    g[x, y, k, self.here(at, RP // 2 * h), :] = s.total(h, 0, at)
+            for k in (0, 1):
+                for d in (1, 2, 3):
+                    rdma(*self.straight(k, d)).wait_recv()
+            for k in (0, 1):
+                rows = pl.ds(self.p * RP, RP)
+                total = g[x, y, k, rows]
+                for d in range(3):
+                    total = total + land2[self.p, k, d]
+                g[x, y, k, rows] = total
 
             rows = pl.ds(self.p * RP, RP)
-            start(g.at[x, y, 1 - zl, rows], zbuf.at[self.p], self.base + 48, dev_zl)
+            start(g.at[x, y, 1 - zl, rows], zbuf.at[self.p], self.base + 30, dev_zl)
 
         def out(self):
             rows = pl.ds(self.p * RP, RP)
-            rdma(g.at[x, y, 1 - zl, rows], zbuf.at[self.p], self.base + 48, dev_zl).wait_recv()
+            rdma(g.at[x, y, 1 - zl, rows], zbuf.at[self.p], self.base + 30, dev_zl).wait_recv()
             obuf[self.p] = (g[x, y, zl, rows] + zbuf[self.p]).astype(BF16)
             src, dst = obuf.at[self.p], obuf_in.at[self.p]
 
@@ -572,7 +583,7 @@
 
             @pl.when(jnp.logical_not(is_self))
             def _():
-                rdma(src, dst, self.base + 49, owner).start()
+                rdma(src, dst, self.base + 31, owner).start()
 
         def done(self):
             src, dst = obuf.at[self.p], obuf_in.at[self.p]
@@ -583,7 +594,7 @@
 
             @pl.when(jnp.logical_not(is_self))
             def _():
-                rdma(src, dst, self.base + 49, owner).wait()
+                rdma(src, dst, self.base + 31, owner).wait()
 
             grad_out[self.p * RP : (self.p + 1) * RP, :] = obuf_in[self.p]
 
@@ -595,8 +606,8 @@
     ga.begin()
     softmax(1)
     ga.backward(0)
+    ga.near()
     gradient(1)
-    ga.near()
     gb.begin()
     ga.backward(3, 1)
     ga.far()
@@ -606,18 +617,16 @@
     ea.relay(ea.one)
     gb.near()
     ea.end_one()
-    ea.begin(ea.two)
+    ea.begin_two()
     gb.backward(3, 1)
     gb.far()
-    ea.relay(ea.two)
     gb.backward(2)
     eb.begin(eb.one)
     ea.end_two()
     eb.relay(eb.one)
     ea.out()
     eb.end_one()
-    eb.begin(eb.two)
-    eb.relay(eb.two)
+    eb.begin_two()
     eb.end_two()
     eb.out()
     ea.done()
@@ -633,7 +642,7 @@
             peer_copy(p, r).wait_send()
 
 
-NSEM = 34 + 8 * NP + 12 * NP + 9 * NP + 50 * NP
+NSEM = 34 + 8 * NP + 12 * NP + 9 * NP + 32 * NP
 
 
 def body(hidden, head, targets, loss_weight):
@@ -663,8 +672,8 @@
             pltpu.VMEM((RING, 2, ROWS, VL), BF16),
             pltpu.VMEM((RING, RING, 2, *tile), F32),
             pltpu.VMEM((NP, 2, 2, 6, 2, RP, WIDTH), I16),
-            pltpu.VMEM((NP, 2, 2, 6, 1, RP // 2, WIDTH), I16),
-            pltpu.VMEM((NP, 5, 2, 6, 8, 128), F32),
+            pltpu.VMEM((NP, 2, 3, RP, WIDTH), F32),
+            pltpu.VMEM((NP, 3, 2, 6, 8, 128), F32),
             pltpu.VMEM((3, 6, 128, 128), F32),
             pltpu.VMEM((NP, RP, WIDTH), F32),
             pltpu.VMEM((NP, RP, WIDTH), BF16),

time: 163 us -> 156 us (0.957)
  Pallas kernels: 158 us -> 151 us
    pallas_call x1, Pallas kernels: 158 us -> 151 us  [body(): pl.pallas_call(kernel, out_shape=(jax.ShapeDtypeStruct((2, ROWS // 2), F3...]
where the time goes in v4:
time: 156 us
  Pallas kernels  151 us (97%)
  local copies, waits for them, and re-layouts  4.24 us (3%)
    pallas_call x1, Pallas kernels, body(): pl.pallas_call(kernel, out_shape=(jax.ShapeDtypeStruct((2, ROWS // 2), F3...  151 us

profile of v4, /device:TPU:37, one launch (start us, length us, event | category | flops | bytes accessed | tf_op | source)
XLA Modules:
  0.0 155.6 jit_solution(4806130572268730665)
XLA Ops:
  0.6 1.5 reshape.10.hid
  2.2 150.7 %mtp_loss.1 = (f32[2,64]{1,0:T(2,128)}, bf16[128,224]{1,0:T(8,128)(2,1)}) custom-call(bf16[128,224]{1,0:T(8,128)(2,1)} %reshape.10.hid, bf16[896,2048]{1,0:T(8,128)(2,1)} %head_hbm.1, s32[2,64]{1,0:T(2,128)} %bitcast.3, f32[2,64]{1,0:T(2,128)} %bitcast.4), custom_call_target="tpu_custom_call" | custom-call | tf_op jit(solution)/shard_map/mtp_loss/pallas_call | solution.py:651
  152.9 1.5 reshape.11
  154.4 1.2 copy.7

commit v5 on v4

--- a/solution.py
+++ b/solution.py
@@ -15,6 +15,7 @@
 HV = VL // 2
 SLAB = 4 * WIDTH
 NP = 2
+PLAIN = (0,)
 RP = ROWS // NP
 I16 = jnp.int16
 LEVELS = 32766.0
@@ -86,6 +87,33 @@
     def total(self, h, t, at):
         i, j = ((3, 4), (2, 5))[h]
         return self.value(0, h, t, at) + self.decoded(i, t, at) + self.decoded(j, t, at)
+
+
+class PlainSum(Ring4Sum):
+    def __init__(self, k, base, part, land, plus, minus):
+        self.k, self.base, self.part, self.land = k, base, part, land
+        self.plus, self.minus = plus, minus
+
+    def copies(self, i):
+        d, h, to_plus = HOPS[i]
+        dev = self.plus if to_plus else self.minus
+        return (self.k.rdma(self.part(d, h), self.land.at[i], self.base + 2 * i, dev),)
+
+    def send(self, i, landed=()):
+        part = self.part(*HOPS[i][:2])
+        for j in landed:
+            part[...] = part[...] + self.land[j]
+        for cp in self.copies(i):
+            cp.start()
+            self.k.pending.append(cp)
+
+    def receive(self, i):
+        for cp in self.copies(i):
+            cp.wait_recv()
+
+    def total(self, h, t, at):
+        i, j = ((3, 4), (2, 5))[h]
+        return self.part(0, h)[t, at, :] + self.land[i, t, at, :] + self.land[j, t, at, :]
 
 
 class Tools:
@@ -130,12 +158,13 @@
     dl,
     g,
     code1,
+    land1,
     land2,
     sides,
     cols,
     zbuf,
     obuf,
-    obuf_in,
+    flat,
     ssem,
     rsem,
     st_s,
@@ -176,6 +205,11 @@
     def greet(dev):
         pl.semaphore_signal(barrier, inc=1, device_id=dev, device_id_type=pl.DeviceIdType.MESH)
 
+    @pl.when(jnp.logical_not(is_self))
+    def _():
+        greet(holder)
+        greet(owner)
+
     for dev in (
         partner,
         dev_zh(1),
@@ -188,10 +222,10 @@
     ):
         greet(dev)
 
+    flat[...] = hid[...].reshape(ROWS, WIDTH)
+
     @pl.when(jnp.logical_not(is_self))
     def _():
-        greet(holder)
-        greet(owner)
         pl.semaphore_wait(barrier, 10)
 
     @pl.when(is_self)
@@ -200,16 +234,16 @@
 
     @pl.when(is_self)
     def _():
-        cp = pltpu.make_async_copy(hid, buf.at[x, y, zl], lsem.at[1])
+        cp = pltpu.make_async_copy(flat, buf.at[x, y, zl], lsem.at[1])
         cp.start()
         cp.wait()
 
     @pl.when(jnp.logical_not(is_self))
     def _():
-        cp = rdma(hid, buf.at[hx, hy, zl], 0, holder)
+        cp = rdma(flat, buf.at[hx, hy, zl], 0, holder)
         cp.start()
         cp.wait_send()
-        rdma(hid, buf.at[x, y, zl], 0, holder).wait_recv()
+        rdma(flat, buf.at[x, y, zl], 0, holder).wait_recv()
 
     start(buf.at[x, y, zl], buf.at[x, y, zl], 1, dev_zl)
 
@@ -222,17 +256,11 @@
 
     tcol[...] = as_column(tgt[...].astype(F32)).astype(jnp.int32)
     wcol[...] = as_column(wgt[...])
-
-    rdma(buf.at[x, y, zl], buf.at[x, y, 1 - zl], 1, dev_zl).wait_recv()
 
     lines = (
         (lambda a, b: buf.at[a, b, 0], x, y, dev_x, dev_y),
         (lambda a, b: buf.at[b, a, 1], y, x, dev_y, dev_x),
     )
-    for k, (at, a, b, dev_a, dev_b) in enumerate(lines):
-        base = 2 + 16 * k
-        for d in (1, 3):
-            start(at(a, b), at(a, b), base + (0 if d == 1 else 1), dev_a(d))
     steps = (0, 3, 1, 2)
 
     def second(k, n):
@@ -249,8 +277,25 @@
         rdma(tile, tile, base + (4 if d == 1 else 8) + n, dev_b(d)).wait_recv()
         return tile
 
+    def first(k):
+        at, a, b, dev_a, dev_b = lines[k]
+        base = 2 + 16 * k
+        tile = at(a, b)
+        return [
+            rdma(tile, tile, base + i, dev)
+            for i, dev in ((0, dev_a(1)), (1, dev_a(3)), (4, dev_b(1)), (8, dev_b(3)))
+        ]
+
+    def start_first(k):
+        for cp in first(k):
+            cp.start()
+
     for k in (0, 1):
-        second(k, 0)
+        kit.pending.extend(first(k))
+        pl.when(zl == k)(lambda: start_first(k))
+    rdma(buf.at[x, y, zl], buf.at[x, y, 1 - zl], 1, dev_zl).wait_recv()
+    for k in (1, 0):
+        pl.when(zl != k)(lambda: start_first(k))
     for k, (at, a, b, dev_a, dev_b) in enumerate(lines):
         base = 2 + 16 * k
         for d, i, rows in ((1, 0, pl.ds(0, 64)), (3, 1, pl.ds(64, 64))):
@@ -517,8 +562,29 @@
                     dev(3),
                 )
 
+            rows = pl.ds(p * RP, RP)
+            if p in PLAIN:
+                self.one = (
+                    PlainSum(
+                        kit,
+                        base,
+                        lambda d, h: g.at[pl.ds(up(2 * h, 2 * zh), 2), up(y, d), 0, rows],
+                        land1.at[p, 0],
+                        dev_y(1),
+                        dev_y(3),
+                    ),
+                    PlainSum(
+                        kit,
+                        base + 12,
+                        lambda d, h: g.at[up(x, d), pl.ds(2 * h, 2), 1, rows],
+                        land1.at[p, 1],
+                        dev_x(1),
+                        dev_x(3),
+                    ),
+                )
+                return
             self.one = (
-                ring(0, 0, lambda d, h, t, at: g[2 * h + t, up(y, d), 0, here(at), :], 2, RP, code1, dev_y),
+                ring(0, 0, lambda d, h, t, at: g[up(2 * h + t, 2 * zh), up(y, d), 0, here(at), :], 2, RP, code1, dev_y),
                 ring(1, 1, lambda d, h, t, at: g[up(x, d), 2 * h + t, 1, here(at), :], 2, RP, code1, dev_x),
             )
 
@@ -540,6 +606,17 @@
                 for s in stage:
                     s.send(i)
 
+        def begin_early(self):
+            for i in (0, 3):
+                self.one[0].send(i)
+
+        def begin_late(self):
+            self.one[0].send(1)
+            self.one[1].send(0)
+            self.one[0].send(2)
+            for i in (1, 2, 3):
+                self.one[1].send(i)
+
         def relay(self, stage):
             for s in stage:
                 s.relay()
@@ -553,7 +630,7 @@
                     for t in (0, 1):
                         val = s.total(h, t, at)
                         if k == 0:
-                            g[2 * h + t, y, 0, self.here(at), :] = val
+                            g[up(2 * h + t, 2 * zh), y, 0, self.here(at), :] = val
                         else:
                             g[x, 2 * h + t, 1, self.here(at), :] = val
 
@@ -575,7 +652,7 @@
             rows = pl.ds(self.p * RP, RP)
             rdma(g.at[x, y, 1 - zl, rows], zbuf.at[self.p], self.base + 30, dev_zl).wait_recv()
             obuf[self.p] = (g[x, y, zl, rows] + zbuf[self.p]).astype(BF16)
-            src, dst = obuf.at[self.p], obuf_in.at[self.p]
+            src, dst = obuf.at[self.p], grad_out.at[rows]
 
             @pl.when(is_self)
             def _():
@@ -586,7 +663,8 @@
                 rdma(src, dst, self.base + 31, owner).start()
 
         def done(self):
-            src, dst = obuf.at[self.p], obuf_in.at[self.p]
+            rows = pl.ds(self.p * RP, RP)
+            src, dst = obuf.at[self.p], grad_out.at[rows]
 
             @pl.when(is_self)
             def _():
@@ -595,8 +673,6 @@
             @pl.when(jnp.logical_not(is_self))
             def _():
                 rdma(src, dst, self.base + 31, owner).wait()
-
-            grad_out[self.p * RP : (self.p + 1) * RP, :] = obuf_in[self.p]
 
     ga, gb = Gather(0), Gather(1)
     ea, eb = Collect(0), Collect(1)
@@ -620,8 +696,9 @@
     ea.begin_two()
     gb.backward(3, 1)
     gb.far()
+    eb.begin_early()
     gb.backward(2)
-    eb.begin(eb.one)
+    eb.begin_late()
     ea.end_two()
     eb.relay(eb.one)
     ea.out()
@@ -655,7 +732,7 @@
             jax.ShapeDtypeStruct(tile, BF16),
         ),
         in_specs=[vmem, pl.BlockSpec(memory_space=pl.ANY), vmem, vmem],
-        out_specs=(vmem, vmem),
+        out_specs=(vmem, pl.BlockSpec(memory_space=pl.ANY)),
         scratch_shapes=[
             pltpu.VMEM((RING, RING, 2, *tile), BF16),
             pltpu.VMEM((SLAB, VL), BF16),
@@ -672,12 +749,13 @@
             pltpu.VMEM((RING, 2, ROWS, VL), BF16),
             pltpu.VMEM((RING, RING, 2, *tile), F32),
             pltpu.VMEM((NP, 2, 2, 6, 2, RP, WIDTH), I16),
+            pltpu.VMEM((NP, 2, 6, 2, RP, WIDTH), F32),
             pltpu.VMEM((NP, 2, 3, RP, WIDTH), F32),
             pltpu.VMEM((NP, 3, 2, 6, 8, 128), F32),
             pltpu.VMEM((3, 6, 128, 128), F32),
             pltpu.VMEM((NP, RP, WIDTH), F32),
             pltpu.VMEM((NP, RP, WIDTH), BF16),
-            pltpu.VMEM((NP, RP, WIDTH), BF16),
+            pltpu.VMEM(tile, BF16),
             pltpu.SemaphoreType.DMA((NSEM,)),
             pltpu.SemaphoreType.DMA((NSEM,)),
             pltpu.SemaphoreType.DMA((NP, NV - 1)),
@@ -688,7 +766,7 @@
             collective_id=0, has_side_effects=True, vmem_limit_bytes=60 * 1024 * 1024
         ),
         name="mtp_loss",
-    )(hidden.reshape(tile), head, targets.T, loss_weight.T)
+    )(hidden, head, targets.T, loss_weight.T)
     rows, depths = targets.shape
     return loss.T, grad.reshape(rows, depths, WIDTH)
 

time: 156 us -> 154 us (0.987)
  no operation moved by 1% of the time
where the time goes in v5:
time: 154 us
  Pallas kernels  151 us (98%)
  local copies, waits for them, and re-layouts  2.71 us (2%)
    pallas_call x1, Pallas kernels, body(): pl.pallas_call(kernel, out_shape=(jax.ShapeDtypeStruct((2, ROWS // 2), F3...  151 us

profile of v5, /device:TPU:37, one launch (start us, length us, event | category | flops | bytes accessed | tf_op | source)
XLA Modules:
  0.0 154.0 jit_solution(600102524234891587)
XLA Ops:
  0.6 150.6 %mtp_loss.1 = (f32[2,64]{1,0:T(2,128)}, bf16[128,224]{1,0:T(8,128)(2,1)}) custom-call(bf16[64,2,224]{2,1,0:T(2,128)(2,1)} %hid.1, bf16[896,2048]{1,0:T(8,128)(2,1)} %head_hbm.1, s32[2,64]{1,0:T(2,128)} %bitcast.3, f32[2,64]{1,0:T(2,128)} %bitcast.4), custom_call_target="tpu_custom_call" | custom-call | tf_op jit(solution)/shard_map/mtp_loss/pallas_call | solution.py:728
  151.3 1.5 reshape.7
  152.8 1.2 copy.7

commit v6 on v5

--- a/solution.py
+++ b/solution.py
@@ -674,6 +674,11 @@
             def _():
                 rdma(src, dst, self.base + 31, owner).wait()
 
+    def peers_sent(p):
+        @pl.loop(1, NV)
+        def _(r):
+            peer_copy(p, r).wait_send()
+
     ga, gb = Gather(0), Gather(1)
     ea, eb = Collect(0), Collect(1)
     softmax(0)
@@ -684,6 +689,7 @@
     ga.backward(0)
     ga.near()
     gradient(1)
+    early = len(kit.pending)
     gb.begin()
     ga.backward(3, 1)
     ga.far()
@@ -692,10 +698,15 @@
     gb.backward(0)
     ea.relay(ea.one)
     gb.near()
+    for cp in kit.pending[:early]:
+        cp.wait_send()
+    del kit.pending[:early]
+    peers_sent(0)
     ea.end_one()
     ea.begin_two()
     gb.backward(3, 1)
     gb.far()
+    peers_sent(1)
     eb.begin_early()
     gb.backward(2)
     eb.begin_late()
@@ -711,12 +722,6 @@
 
     for cp in kit.pending:
         cp.wait_send()
-
-    for p in range(NP):
-
-        @pl.loop(1, NV)
-        def _(r):
-            peer_copy(p, r).wait_send()
 
 
 NSEM = 34 + 8 * NP + 12 * NP + 9 * NP + 32 * NP

time: 154 us -> 153 us (level)
  Pallas kernels: 151 us -> 149 us
where the time goes in v6:
time: 153 us
  Pallas kernels  149 us (97%)
  local copies, waits for them, and re-layouts  2.71 us (2%)
    pallas_call x1, Pallas kernels, body(): pl.pallas_call(kernel, out_shape=(jax.ShapeDtypeStruct((2, ROWS // 2), F3...  149 us

profile of v6, /device:TPU:37, one launch (start us, length us, event | category | flops | bytes accessed | tf_op | source)
XLA Modules:
  0.0 152.6 jit_solution(8642055004611977055)
XLA Ops:
  0.6 149.3 %mtp_loss.1 = (f32[2,64]{1,0:T(2,128)}, bf16[128,224]{1,0:T(8,128)(2,1)}) custom-call(bf16[64,2,224]{2,1,0:T(2,128)(2,1)} %hid.1, bf16[896,2048]{1,0:T(8,128)(2,1)} %head_hbm.1, s32[2,64]{1,0:T(2,128)} %bitcast.3, f32[2,64]{1,0:T(2,128)} %bitcast.4), custom_call_target="tpu_custom_call" | custom-call | tf_op jit(solution)/shard_map/mtp_loss/pallas_call | solution.py:733
  149.9 1.5 reshape.7
  151.4 1.2 copy.7

commit v7 on v6

--- a/solution.py
+++ b/solution.py
@@ -697,6 +697,7 @@
     ea.begin(ea.one)
     gb.backward(0)
     ea.relay(ea.one)
+    later = len(kit.pending) - early
     gb.near()
     for cp in kit.pending[:early]:
         cp.wait_send()
@@ -706,6 +707,9 @@
     ea.begin_two()
     gb.backward(3, 1)
     gb.far()
+    for cp in kit.pending[:later]:
+        cp.wait_send()
+    del kit.pending[:later]
     peers_sent(1)
     eb.begin_early()
     gb.backward(2)

time: 153 us -> 153 us (level)
  no operation moved by 1% of the time
where the time goes in v7:
time: 153 us
  Pallas kernels  149 us (97%)
  local copies, waits for them, and re-layouts  2.71 us (2%)
    pallas_call x1, Pallas kernels, body(): pl.pallas_call(kernel, out_shape=(jax.ShapeDtypeStruct((2, ROWS // 2), F3...  149 us

profile of v7, /device:TPU:37, one launch (start us, length us, event | category | flops | bytes accessed | tf_op | source)
XLA Modules:
  0.0 152.6 jit_solution(6235751684144215264)
XLA Ops:
  0.6 149.3 %mtp_loss.1 = (f32[2,64]{1,0:T(2,128)}, bf16[128,224]{1,0:T(8,128)(2,1)}) custom-call(bf16[64,2,224]{2,1,0:T(2,128)(2,1)} %hid.1, bf16[896,2048]{1,0:T(8,128)(2,1)} %head_hbm.1, s32[2,64]{1,0:T(2,128)} %bitcast.3, f32[2,64]{1,0:T(2,128)} %bitcast.4), custom_call_target="tpu_custom_call" | custom-call | tf_op jit(solution)/shard_map/mtp_loss/pallas_call | solution.py:737
  149.9 1.5 reshape.7
  151.4 1.2 copy.7
